TPU v7x, 32 devices: a whole 2x2x4 slice. The times are simulated.
32 devices in a mesh: rep: 4 (over y, x), shard: 8 (over z, core).
Axes of the slice: x: 2, y: 2, z: 4, core: 2. Of those that a mesh axis runs over, the one named last changes fastest.
Arguments:
- tokens: bfloat16 [32, 1024, 768], P(('rep', 'shard')), may hold values from -6 to 6
- segment_ids: int32 [32, 1024], P(('rep', 'shard')), may hold values from 0 to 15, never falling along the last dimension, each value on 1 to 512 neighbouring positions
- qkv_weight: bfloat16 [768, 2304], P(None, 'shard'), may hold values from -0.15605632 to 0.15605632
- out_weight: bfloat16 [768, 768], P('shard'), may hold values from -0.4375 to 0.4375
- up_weight: bfloat16 [768, 3072], P(None, 'shard'), may hold values from -0.21875 to 0.21875
- down_weight: bfloat16 [3072, 768], P('shard'), may hold values from -0.109375 to 0.109375
- norm1_gain: bfloat16 [768], P('shard'), may hold values from 0.5 to 1.5
- norm1_shift: bfloat16 [768], P('shard'), may hold values from -2.5 to 2.5
- norm2_gain: bfloat16 [768], P('shard'), may hold values from 0.5 to 1.5
- norm2_shift: bfloat16 [768], P('shard'), may hold values from -2.5 to 2.5
- cotangent: bfloat16 [32, 1024, 768], P(('rep', 'shard')), may hold values from -6 to 6
Outputs:
- output: bfloat16 [32, 1024, 768], P(('rep', 'shard'))
- tokens_grad: bfloat16 [32, 1024, 768], P(('rep', 'shard'))
- qkv_weight_grad: float32 [768, 2304], P(None, 'shard')
- out_weight_grad: float32 [768, 768], P('shard')
- up_weight_grad: float32 [768, 3072], P(None, 'shard')
- down_weight_grad: float32 [3072, 768], P('shard')
- norm1_gain_grad: float32 [768], P('shard')
- norm1_shift_grad: float32 [768], P('shard')
- norm2_gain_grad: float32 [768], P('shard')
- norm2_shift_grad: float32 [768], P('shard')
Inputs may be any that keep to these rules, and one draw needn't show every extreme that they name: `segment_ids`: within each sequence the ids never fall, every id of 0 to 15 is used, each document is a run of 1 to 512 slots, and the longest document of a draw has exactly 512 slots.
All inputs are finite; a program needn't handle non-finite values.
Results may differ from a plain program's by a relative error of at most 0.015.
Values may be sent and summed in bfloat16 or wider, within the bound.
A program may use at most 256 MiB of HBM per device.

v0:
```python
import jax
import jax.numpy as jnp
from jax import lax
from jax.sharding import PartitionSpec as P

HEADS = 12
HEAD_DIM = 64


norm_eps = 1e-05
masked_value = -1e30
highest = lax.Precision.HIGHEST


def norm_forward(inputs, gain_vec, shift_vec):
    average = jnp.mean(inputs, axis=-1, keepdims=True)
    center = inputs - average
    variance = jnp.mean(center * center, axis=-1, keepdims=True)
    inverse = lax.rsqrt(variance + norm_eps)
    unit_rows = center * inverse
    return (unit_rows * gain_vec + shift_vec, unit_rows, inverse)


def norm_backward(grad_normed, unit_rows, inverse, gain_vec):
    grad_unit = grad_normed * gain_vec
    grad_mean = jnp.mean(grad_unit, axis=-1, keepdims=True)
    grad_proj = jnp.mean(grad_unit * unit_rows, axis=-1, keepdims=True)
    return inverse * (grad_unit - grad_mean - unit_rows * grad_proj)


def gelu_tanh(inputs):
    return jax.nn.gelu(inputs, approximate=True)


def block_masks(segment, starts, row_start, block_rows):
    length = segment.shape[0]
    rows_here = row_start + jnp.arange(block_rows, dtype=jnp.int32)
    columns = jnp.arange(length, dtype=jnp.int32)
    row_segment = lax.dynamic_slice_in_dim(segment, row_start, block_rows)
    same_doc = row_segment[:, None] == segment[None, :]
    allowed = same_doc & (columns[None, :] <= rows_here[:, None])
    chosen = same_doc & (columns[None, :] < rows_here[:, None]) & jnp.logical_not(starts)[None, :]
    return (allowed, chosen)


def block_logits(query_block, key_heads, column_sums, allowed, chosen, below_mask):
    scores = jnp.einsum(
        "qhd,khd->hqk", query_block, key_heads, preferred_element_type=jnp.float32
    ) * HEAD_DIM ** (-0.5)
    select = jnp.where(chosen, jax.nn.softplus(scores[0]), 0.0)
    penalty = column_sums[None, :] + jnp.dot(below_mask, select, precision=highest)
    logits = jnp.where(allowed[None], scores - penalty[None], masked_value)
    return (scores, select, logits)


def strict_below(block_rows):
    steps_up = jnp.arange(block_rows, dtype=jnp.int32)
    return (steps_up[:, None] > steps_up[None, :]).astype(jnp.float32)


def attend_forward(queries, key_heads, values, segment, starts, block_rows):
    length = queries.shape[0]
    below_mask = strict_below(block_rows)

    def block_step(column_sums, block_index):
        row_start = block_index * block_rows
        query_block = lax.dynamic_slice_in_dim(queries, row_start, block_rows, 0)
        allowed, chosen = block_masks(segment, starts, row_start, block_rows)
        scores, select, logits = block_logits(
            query_block, key_heads, column_sums, allowed, chosen, below_mask
        )
        row_peak = jnp.max(logits, axis=-1, keepdims=True)
        exps = jnp.exp(logits - row_peak)
        row_total = jnp.sum(exps, axis=-1, keepdims=True)
        attention = (exps / row_total).astype(jnp.bfloat16)
        attended = jnp.einsum("hqk,khd->qhd", attention, values, preferred_element_type=jnp.float32)
        kept = (
            attended.reshape(block_rows, HEADS * HEAD_DIM),
            row_peak + jnp.log(row_total),
            column_sums,
        )
        return (column_sums + jnp.sum(select, axis=0), kept)

    initial = jnp.zeros((length,), jnp.float32)
    unused, (attended, log_total, carries) = lax.scan(
        block_step, initial, jnp.arange(length // block_rows)
    )
    return (attended.reshape(length, HEADS * HEAD_DIM), log_total, carries)


def attend_backward(
    queries, key_heads, values, grad_attended, segment, starts, block_rows, log_total, carries
):
    length = queries.shape[0]
    below_mask = strict_below(block_rows)
    above_mask = below_mask.T
    grad_heads = grad_attended.reshape(length, HEADS, HEAD_DIM)

    def block_step(back_state, block_index):
        later_sums, grad_keys, grad_values = back_state
        row_start = block_index * block_rows
        query_block = lax.dynamic_slice_in_dim(queries, row_start, block_rows, 0)
        grad_block = lax.dynamic_slice_in_dim(grad_heads, row_start, block_rows, 0)
        allowed, chosen = block_masks(segment, starts, row_start, block_rows)
        scores, select, logits = block_logits(
            query_block, key_heads, carries[block_index], allowed, chosen, below_mask
        )
        attention = jnp.exp(logits - log_total[block_index])
        grad_probs = jnp.einsum(
            "qhd,khd->hqk", grad_block, values, preferred_element_type=jnp.float32
        )
        row_delta = jnp.sum(attention * grad_probs, axis=-1, keepdims=True)
        grad_logits = attention * (grad_probs - row_delta)
        grad_penalty = -jnp.sum(grad_logits, axis=0)
        grad_select = later_sums[None, :] + jnp.dot(above_mask, grad_penalty, precision=highest)
        grad_first = grad_logits[0] + jnp.where(
            chosen, grad_select * jax.nn.sigmoid(scores[0]), 0.0
        )
        grad_scores = jnp.concatenate([grad_first[None], grad_logits[1:]], axis=0).astype(
            jnp.bfloat16
        )
        grad_query = jnp.einsum(
            "hqk,khd->qhd", grad_scores, key_heads, preferred_element_type=jnp.float32
        ) * HEAD_DIM ** (-0.5)
        grad_keys = grad_keys + jnp.einsum(
            "hqk,qhd->khd", grad_scores, query_block, preferred_element_type=jnp.float32
        ) * HEAD_DIM ** (-0.5)
        grad_values = grad_values + jnp.einsum(
            "hqk,qhd->khd",
            attention.astype(jnp.bfloat16),
            grad_block,
            preferred_element_type=jnp.float32,
        )
        return ((later_sums + jnp.sum(grad_penalty, axis=0), grad_keys, grad_values), grad_query)

    empty_heads = jnp.zeros((length, HEADS, HEAD_DIM), jnp.float32)
    initial = (jnp.zeros((length,), jnp.float32), empty_heads, empty_heads)
    final_state, grad_queries = lax.scan(
        block_step, initial, jnp.arange(length // block_rows), reverse=True
    )
    model_width = HEADS * HEAD_DIM
    pieces = [
        grad_queries.reshape(length, model_width),
        final_state[1].reshape(length, model_width),
        final_state[2].reshape(length, model_width),
    ]
    return jnp.concatenate(pieces, axis=1).astype(jnp.bfloat16)


def local(
    tokens,
    segment_ids,
    qkv_weight,
    out_weight,
    up_weight,
    down_weight,
    norm1_gain,
    norm1_shift,
    norm2_gain,
    norm2_shift,
    cotangent,
):
    inputs = tokens[0].astype(jnp.float32)
    segment = segment_ids[0]
    length = inputs.shape[0]
    block_rows = min(512, length)
    model_width = HEADS * HEAD_DIM
    starts = jnp.concatenate([jnp.ones((1,), dtype=bool), segment[1:] != segment[:-1]])
    gathered = (
        lax.all_gather(qkv_weight, "shard", axis=1, tiled=True),
        lax.all_gather(out_weight, "shard", axis=0, tiled=True),
        lax.all_gather(up_weight, "shard", axis=1, tiled=True),
        lax.all_gather(down_weight, "shard", axis=0, tiled=True),
        lax.all_gather(norm1_gain, "shard", axis=0, tiled=True),
        lax.all_gather(norm1_shift, "shard", axis=0, tiled=True),
        lax.all_gather(norm2_gain, "shard", axis=0, tiled=True),
        lax.all_gather(norm2_shift, "shard", axis=0, tiled=True),
    )
    qkv_full, out_full, up_full, down_full, gain_one, shift_one, gain_two, shift_two = gathered
    normed_one, unit_one, inverse_one = norm_forward(
        inputs, gain_one.astype(jnp.float32), shift_one.astype(jnp.float32)
    )
    normed_one = normed_one.astype(jnp.bfloat16)
    projected = jnp.dot(normed_one, qkv_full, preferred_element_type=jnp.float32).astype(
        jnp.bfloat16
    )
    queries = projected[:, :model_width].reshape(length, HEADS, HEAD_DIM)
    key_heads = projected[:, model_width : 2 * model_width].reshape(length, HEADS, HEAD_DIM)
    values = projected[:, 2 * model_width :].reshape(length, HEADS, HEAD_DIM)
    attended, log_total, carries = attend_forward(
        queries, key_heads, values, segment, starts, block_rows
    )
    attended = attended.astype(jnp.bfloat16)
    residual = inputs + jnp.dot(attended, out_full, preferred_element_type=jnp.float32)
    normed_two, unit_two, inverse_two = norm_forward(
        residual, gain_two.astype(jnp.float32), shift_two.astype(jnp.float32)
    )
    normed_two = normed_two.astype(jnp.bfloat16)
    hidden = jnp.dot(normed_two, up_full, preferred_element_type=jnp.float32)
    active = gelu_tanh(hidden).astype(jnp.bfloat16)
    output = residual + jnp.dot(active, down_full, preferred_element_type=jnp.float32)
    regathered = (
        lax.all_gather(qkv_weight, "shard", axis=1, tiled=True),
        lax.all_gather(out_weight, "shard", axis=0, tiled=True),
        lax.all_gather(up_weight, "shard", axis=1, tiled=True),
        lax.all_gather(down_weight, "shard", axis=0, tiled=True),
        lax.all_gather(norm1_gain, "shard", axis=0, tiled=True),
        lax.all_gather(norm1_shift, "shard", axis=0, tiled=True),
        lax.all_gather(norm2_gain, "shard", axis=0, tiled=True),
        lax.all_gather(norm2_shift, "shard", axis=0, tiled=True),
    )
    qkv_full, out_full, up_full, down_full, gain_one, shift_one, gain_two, shift_two = regathered
    grad_out = cotangent[0]
    grad_down = jnp.einsum("tf,td->fd", active, grad_out, preferred_element_type=jnp.float32)
    grad_active = jnp.einsum("td,fd->tf", grad_out, down_full, preferred_element_type=jnp.float32)
    unused, gelu_pullback = jax.vjp(gelu_tanh, hidden)
    grad_hidden = gelu_pullback(grad_active)[0].astype(jnp.bfloat16)
    grad_up = jnp.einsum("td,tf->df", normed_two, grad_hidden, preferred_element_type=jnp.float32)
    grad_normed_two = jnp.einsum(
        "tf,df->td", grad_hidden, up_full, preferred_element_type=jnp.float32
    )
    gain_two_grad = jnp.sum(grad_normed_two * unit_two, axis=0)
    shift_two_grad = jnp.sum(grad_normed_two, axis=0)
    grad_residual = grad_out.astype(jnp.float32) + norm_backward(
        grad_normed_two, unit_two, inverse_two, gain_two.astype(jnp.float32)
    )
    grad_branch = grad_residual.astype(jnp.bfloat16)
    grad_outw = jnp.einsum("tc,td->cd", attended, grad_branch, preferred_element_type=jnp.float32)
    grad_attended = jnp.einsum(
        "td,cd->tc", grad_branch, out_full, preferred_element_type=jnp.float32
    ).astype(jnp.bfloat16)
    grad_projected = attend_backward(
        queries, key_heads, values, grad_attended, segment, starts, block_rows, log_total, carries
    )
    grad_qkvw = jnp.einsum(
        "td,te->de", normed_one, grad_projected, preferred_element_type=jnp.float32
    )
    grad_normed_one = jnp.einsum(
        "te,de->td", grad_projected, qkv_full, preferred_element_type=jnp.float32
    )
    gain_one_grad = jnp.sum(grad_normed_one * unit_one, axis=0)
    shift_one_grad = jnp.sum(grad_normed_one, axis=0)
    grad_tokens = grad_residual + norm_backward(
        grad_normed_one, unit_one, inverse_one, gain_one.astype(jnp.float32)
    )
    shares = (
        lax.psum_scatter(grad_qkvw, "shard", scatter_dimension=1, tiled=True),
        lax.psum_scatter(grad_outw, "shard", scatter_dimension=0, tiled=True),
        lax.psum_scatter(grad_up, "shard", scatter_dimension=1, tiled=True),
        lax.psum_scatter(grad_down, "shard", scatter_dimension=0, tiled=True),
        lax.psum_scatter(gain_one_grad, "shard", scatter_dimension=0, tiled=True),
        lax.psum_scatter(shift_one_grad, "shard", scatter_dimension=0, tiled=True),
        lax.psum_scatter(gain_two_grad, "shard", scatter_dimension=0, tiled=True),
        lax.psum_scatter(shift_two_grad, "shard", scatter_dimension=0, tiled=True),
    )
    totals = (
        lax.psum(shares[0].astype(jnp.bfloat16), "rep").astype(jnp.float32),
        lax.psum(shares[1].astype(jnp.bfloat16), "rep").astype(jnp.float32),
        lax.psum(shares[2].astype(jnp.bfloat16), "rep").astype(jnp.float32),
        lax.psum(shares[3].astype(jnp.bfloat16), "rep").astype(jnp.float32),
        lax.psum(shares[4].astype(jnp.bfloat16), "rep").astype(jnp.float32),
        lax.psum(shares[5].astype(jnp.bfloat16), "rep").astype(jnp.float32),
        lax.psum(shares[6].astype(jnp.bfloat16), "rep").astype(jnp.float32),
        lax.psum(shares[7].astype(jnp.bfloat16), "rep").astype(jnp.float32),
    )
    return (
        output.astype(jnp.bfloat16)[None],
        grad_tokens.astype(jnp.bfloat16)[None],
        totals[0],
        totals[1],
        totals[2],
        totals[3],
        totals[4],
        totals[5],
        totals[6],
        totals[7],
    )


def solution(mesh):
    placed = (
        P(("rep", "shard"), None, None),
        P(("rep", "shard"), None),
        P(None, "shard"),
        P("shard", None),
        P(None, "shard"),
        P("shard", None),
        P("shard"),
        P("shard"),
        P("shard"),
        P("shard"),
        P(("rep", "shard"), None, None),
    )
    return jax.shard_map(
        local,
        mesh=mesh,
        in_specs=placed,
        out_specs=(
            P(("rep", "shard"), None, None),
            P(("rep", "shard"), None, None),
            P(None, "shard"),
            P("shard", None),
            P(None, "shard"),
            P("shard", None),
            P("shard"),
            P("shard"),
            P("shard"),
            P("shard"),
        ),
        check_vma=False,
    )
```

profile of v0, /device:TPU:0, one launch (start us, length us, event | category | flops | bytes accessed | tf_op | source)
XLA Modules:
  0.0 860.1 jit_solution(2461581973469124994)
XLA Ops:
  15.5 19.2 %all-reduce.9 = (bf16[768]{0:T(1024)(128)(2,1)S(1)}, bf16[768]{0:T(1024)(128)(2,1)S(1)}, bf16[768]{0:T(1024)(128)(2,1)S(1)}, bf16[768]{0:T(1024)(128)(2,1)S(1)}) all-reduce(bf16[768]{0:T(1024)(128)(2,1)S(1)} %dynamic-update-slice.1, bf16[768]{0:T(1024)(128)(2,1)S(1)} %dynamic-update-slice, ...), channel_id=1, replica_groups=mesh['rep'=4,'shard'=8] {'shard'}, use_global_device_ids=true, to_apply=%add.1 | all-reduce | flops 3072 | bytes 12288
  41.1 13.3 %all-gather.5.cloned.1.call-done = bf16[768,2304]{0,1:T(8,128)(2,1)} async-done(((bf16[768,288]{0,1:T(8,128)(2,1)}), bf16[768,2304]{0,1:T(8,128)(2,1)}) %all-gather.5.cloned.1.call-update) | async-done | bytes 3538960 | tf_op jit(solution)/shard_map/all_gather | solution.py:170
  68.3 128.3 %while.40 = (s32[]{:T(128)}, f32[1024]{0:T(1024)S(1)}, bf16[2,512,768]{2,1,0:T(8,128)(2,1)}, f32[2,12,512,1]{2,1,3,0:T(8,128)}, f32[2,1024]{1,0:T(2,128)S(1)}, /...) while((s32[]{:T(128)}, f32[1024]{0:T(1024)S(1)}, ...), condition=%wide.region_6.7_spmd.clone, body=%wide.region_2.6_spmd.clone.sunk | while | flops 4928302592 | bytes 335702400 | solution.py:85
  75.6 8.3 copy-done
  85.7 11.2 %add_bitcast_fusion.4 = f32[512,1024]{0,1:T(8,128)} fusion(f32[1024]{0:T(1024)S(1)} %get-tuple-element.909, f32[12,512,1024]{2,1,0:T(8,128)} %copy-done, s32[512]{0:T(512)S(1)} %iota_add_fusion.4, s32[1024]{0:T(1024)S(1)} %bitcast.207, s32[512]{0:T(512)S(1)} %dynamic_slice.106, pred[1024]{0:T(1024)(128)(4,1)S(1)} %reduce.6), kind=kOutput, calls=%fused_computation.15.clone.1 | convolution fusion | flops 3228041216 | bytes 4207616 | tf_op jit(solution)/shard_map/while/body/eval_jaxpr/dot_general | solution.py:51
  98.8 11.3 %fusion.162 = f32[12,512]{1,0:T(8,128)S(1)} fusion(f32[12,512,1024]{2,1,0:T(8,128)} %copy-done, f32[512,1024]{1,0:T(8,128)S(1)} %copy.93, pred[512,1024]{1,0:T(8,128)(4,1)S(1)} %compare_and_fusion.6), kind=kLoop, calls=%fused_computation.6.clone.1 | loop fusion | flops 18868224 | bytes 27811840 | tf_op jit(solution)/shard_map/while/body/eval_jaxpr/reduce_max | solution.py:72
  139.5 8.4 copy-done
  149.8 11.1 %add_bitcast_fusion.4 = f32[512,1024]{0,1:T(8,128)} fusion(f32[1024]{0:T(1024)S(1)} %get-tuple-element.909, f32[12,512,1024]{2,1,0:T(8,128)} %copy-done, s32[512]{0:T(512)S(1)} %iota_add_fusion.4, s32[1024]{0:T(1024)S(1)} %bitcast.207, s32[512]{0:T(512)S(1)} %dynamic_slice.106, pred[1024]{0:T(1024)(128)(4,1)S(1)} %reduce.6), kind=kOutput, calls=%fused_computation.15.clone.1 | convolution fusion | flops 3228041216 | bytes 4207616 | tf_op jit(solution)/shard_map/while/body/eval_jaxpr/dot_general | solution.py:51
  162.7 11.3 %fusion.162 = f32[12,512]{1,0:T(8,128)S(1)} fusion(f32[12,512,1024]{2,1,0:T(8,128)} %copy-done, f32[512,1024]{1,0:T(8,128)S(1)} %copy.93, pred[512,1024]{1,0:T(8,128)(4,1)S(1)} %compare_and_fusion.6), kind=kLoop, calls=%fused_computation.6.clone.1 | loop fusion | flops 18868224 | bytes 27811840 | tf_op jit(solution)/shard_map/while/body/eval_jaxpr/reduce_max | solution.py:72
  201.2 10.9 %fusion.107 = f32[1024,3072]{1,0:T(8,128)} fusion(bf16[768,3072]{1,0:T(8,128)(2,1)} %all-gather.9.cloned.1.call-done, f32[1024,768]{0,1:T(8,128)S(1)} %get-tuple-element.743, f32[768]{0:T(1024)S(1)} %copy-done.38, f32[768]{0:T(1024)S(1)} %copy-done.32, f32[1024]{0:T(1024)S(1)} %add_rsqrt_fusion, f32[1024]{0:T(1024)S(1)} %broadcast_multiply_fusion.6), kind=kOutput, calls=%fused_computation.162 | convolution fusion | flops 4835770368 | bytes 20461568 | tf_op jit(solution)/shard_map/dot_general | solution.py:199
  212.1 15.7 %fusion.74 = bf16[1024,3072]{1,0:T(8,128)(2,1)S(1)} fusion(f32[1024,3072]{1,0:T(8,128)} %fusion.107, bf16[3072,768]{1,0:T(8,128)(2,1)} %all-gather.11.cloned.1.call-done, bf16[1,1024,768]{2,1,0:T(8,128)(2,1)} %param.25), kind=kOutput, calls=%fused_computation.102 | convolution fusion | flops 4894752768 | bytes 25165824 | tf_op jit(solution)/shard_map/td,fd->tf/dot_general | solution.py:215
  253.7 234.1 %while.41 = (s32[]{:T(128)}, f32[1024]{0:T(1024)S(1)}, f32[1024,12,64]{0,2,1:T(8,128)}, f32[1024,12,64]{0,2,1:T(8,128)}, bf16[2,512,12,64]{1,3,2,0:T(8,128)(2,1)...) while((s32[]{:T(128)}, f32[1024]{0:T(1024)S(1)}, ...), condition=%wide.region_15.16_spmd.clone, body=%wide.region_11.15_spmd.clone.sunk | while | flops 10608046080 | bytes 423868928 | solution.py:138
  263.8 8.5 copy-done.2
  272.3 9.5 %add_bitcast_fusion.5 = f32[512,1024]{0,1:T(8,128)} fusion(f32[12,512,1024]{2,1,0:T(8,128)S(1)} %broadcast_multiply_fusion.11, f32[1024]{0:T(1024)S(1)} %bitcast.222, s32[512]{0:T(512)S(1)} %iota_add_fusion.5, s32[1024]{0:T(1024)S(1)} %bitcast.212, s32[512]{0:T(512)S(1)} %dynamic_slice.114, pred[1024]{0:T(1024)(128)(4,1)S(1)} %reduce.7), kind=kOutput, calls=%fused_computation.55.clone.1 | convolution fusion | flops 3228041216 | bytes 4207616 | tf_op jit(solution)/shard_map/while/body/eval_jaxpr/dot_general | solution.py:51
  283.7 13.7 %bitcast_add_fusion.5 = f32[1024,12,64]{0,2,1:T(8,128)} fusion(f32[1024,12,64]{0,2,1:T(8,128)} %get-tuple-element.1007, f32[12,512,1024]{2,1,0:T(8,128)} %copy-done.2, f32[12,512]{1,0:T(8,128)S(1)} %dynamic-slice_bitcast_fusion.2, f32[512,1024]{1,0:T(8,128)S(1)} %copy.95, pred[512,1024]{1,0:T(8,128)(4,1)S(1)} %compare_and_fusion.7, ...), kind=kOutput, calls=%fused_computation.41.clone.1 | convolution fusion | flops 832045056 | bytes 34889732 | tf_op jit(solution)/shard_map/while/body/eval_jaxpr/hqk,qhd->khd/dot_general | solution.py:128
  297.5 18.3 %multiply_reduce_fusion.7 = (f32[12,512]{1,0:T(8,128)S(1)}, f32[12,512,1024]{2,1,0:T(8,128)}) fusion(f32[12,512,1024]{2,1,0:T(8,128)} %copy-done.2, f32[12,512]{1,0:T(8,128)S(1)} %dynamic-slice_bitcast_fusion.2, f32[512,1024]{1,0:T(8,128)S(1)} %copy.95, pred[512,1024]{1,0:T(8,128)(4,1)S(1)} %compare_and_fusion.7, ...), kind=kOutput, calls=%fused_computation.30.clone.1 | convolution fusion | flops 836757504 | bytes 55361540 | tf_op jit(solution)/shard_map/while/body/eval_jaxpr/qhd,khd->hqk/dot_general | solution.py:109
  315.8 25.2 %fusion.176 = (f32[512,1024]{1,0:T(8,128)S(1)}, f32[1024]{0:T(1024)S(1)}, f32[12,512,1024]{2,1,0:T(8,128)}) fusion(f32[12,512,1024]{2,1,0:T(8,128)} %get-tuple-element.925, f32[12,512]{1,0:T(8,128)S(1)} %get-tuple-element.926, f32[12,512]{1,0:T(8,128)S(1)} %dynamic-slice_bitcast_fusion.2, f32[12,512,1024]{2,1,0:T(8,128)} %copy-done.2, ...), kind=kLoop, calls=%fused_computation.163.clone.1 | loop fusion | flops 43514880 | bytes 80269312 | tf_op jit(solution)/shard_map/while/body/eval_jaxpr/reduce_sum | solution.py:114
  347.7 9.5 %slice.108 = bf16[11,512,1024]{2,1,0:T(8,128)(2,1)S(1)} slice(f32[12,512,1024]{2,1,0:T(8,128)} %get-tuple-element.929), slice={[1:12], [0:512], [0:1024]} | slice | bytes 23068672 | tf_op jit(solution)/shard_map/while/body/eval_jaxpr/slice | solution.py:119
  384.4 9.5 %add_bitcast_fusion.5 = f32[512,1024]{0,1:T(8,128)} fusion(f32[12,512,1024]{2,1,0:T(8,128)S(1)} %broadcast_multiply_fusion.11, f32[1024]{0:T(1024)S(1)} %bitcast.222, s32[512]{0:T(512)S(1)} %iota_add_fusion.5, s32[1024]{0:T(1024)S(1)} %bitcast.212, s32[512]{0:T(512)S(1)} %dynamic_slice.114, pred[1024]{0:T(1024)(128)(4,1)S(1)} %reduce.7), kind=kOutput, calls=%fused_computation.55.clone.1 | convolution fusion | flops 3228041216 | bytes 4207616 | tf_op jit(solution)/shard_map/while/body/eval_jaxpr/dot_general | solution.py:51
  395.8 14.6 %bitcast_add_fusion.5 = f32[1024,12,64]{0,2,1:T(8,128)} fusion(f32[1024,12,64]{0,2,1:T(8,128)} %get-tuple-element.1007, f32[12,512,1024]{2,1,0:T(8,128)} %copy-done.2, f32[12,512]{1,0:T(8,128)S(1)} %dynamic-slice_bitcast_fusion.2, f32[512,1024]{1,0:T(8,128)S(1)} %copy.95, pred[512,1024]{1,0:T(8,128)(4,1)S(1)} %compare_and_fusion.7, ...), kind=kOutput, calls=%fused_computation.41.clone.1 | convolution fusion | flops 832045056 | bytes 34889732 | tf_op jit(solution)/shard_map/while/body/eval_jaxpr/hqk,qhd->khd/dot_general | solution.py:128
  410.5 18.3 %multiply_reduce_fusion.7 = (f32[12,512]{1,0:T(8,128)S(1)}, f32[12,512,1024]{2,1,0:T(8,128)}) fusion(f32[12,512,1024]{2,1,0:T(8,128)} %copy-done.2, f32[12,512]{1,0:T(8,128)S(1)} %dynamic-slice_bitcast_fusion.2, f32[512,1024]{1,0:T(8,128)S(1)} %copy.95, pred[512,1024]{1,0:T(8,128)(4,1)S(1)} %compare_and_fusion.7, ...), kind=kOutput, calls=%fused_computation.30.clone.1 | convolution fusion | flops 836757504 | bytes 55361540 | tf_op jit(solution)/shard_map/while/body/eval_jaxpr/qhd,khd->hqk/dot_general | solution.py:109
  428.8 25.2 %fusion.176 = (f32[512,1024]{1,0:T(8,128)S(1)}, f32[1024]{0:T(1024)S(1)}, f32[12,512,1024]{2,1,0:T(8,128)}) fusion(f32[12,512,1024]{2,1,0:T(8,128)} %get-tuple-element.925, f32[12,512]{1,0:T(8,128)S(1)} %get-tuple-element.926, f32[12,512]{1,0:T(8,128)S(1)} %dynamic-slice_bitcast_fusion.2, f32[12,512,1024]{2,1,0:T(8,128)} %copy-done.2, ...), kind=kLoop, calls=%fused_computation.163.clone.1 | loop fusion | flops 43514880 | bytes 80269312 | tf_op jit(solution)/shard_map/while/body/eval_jaxpr/reduce_sum | solution.py:114
  460.7 9.5 %slice.108 = bf16[11,512,1024]{2,1,0:T(8,128)(2,1)S(1)} slice(f32[12,512,1024]{2,1,0:T(8,128)} %get-tuple-element.929), slice={[1:12], [0:512], [0:1024]} | slice | bytes 23068672 | tf_op jit(solution)/shard_map/while/body/eval_jaxpr/slice | solution.py:119
  503.2 12.4 %fusion.95 = f32[3072,768]{1,0:T(8,128)} fusion(bf16[1,1024,768]{2,1,0:T(8,128)(2,1)S(1)} %copy-done.23, f32[1024,3072]{1,0:T(8,128)} %fusion.107), kind=kOutput, calls=%fused_computation.138 | convolution fusion | flops 4860149760 | bytes 23592960 | tf_op jit(solution)/shard_map/tf,td->fd/dot_general | solution.py:214
  517.5 10.5 %fusion.106 = f32[768,3072]{1,0:T(8,128)} fusion(bf16[1024,3072]{1,0:T(8,128)(2,1)} %copy-done.53, f32[1024,768]{0,1:T(8,128)S(1)} %copy-done.7, f32[768]{0:T(1024)S(1)} %copy-done.39, f32[768]{0:T(1024)S(1)} %copy-done.33, f32[1024]{0:T(1024)S(1)} %copy-done.35, f32[1024]{0:T(1024)S(1)} %copy-done.30), kind=kOutput, calls=%fused_computation.161 | convolution fusion | flops 4835770368 | bytes 18888704 | tf_op jit(solution)/shard_map/td,tf->df/dot_general | solution.py:218
  529.0 11.3 %fusion.98 = bf16[1,1024,768]{1,2,0:T(8,128)(2,1)} fusion(f32[1024,768]{0,1:T(8,128)S(1)} %copy-done.7, bf16[3072,768]{1,0:T(8,128)(2,1)} %all-gather.11.cloned.1.call-done, f32[1024,3072]{1,0:T(8,128)} %fusion.107), kind=kOutput, calls=%fused_computation.141 | convolution fusion | flops 4861722624 | bytes 22020096 | tf_op jit(solution)/shard_map/dot_general | solution.py:201
  542.0 36.6 %reduce-scatter.5.cloned.1.call-done = f32[768,288]{0,1:T(8,128)} async-done(((f32[768,2304]{0,1:T(8,128)}), f32[768,288]{0,1:T(8,128)}) %reduce-scatter.5.cloned.1.call-update) | async-done | bytes 884752 | tf_op jit(solution)/shard_map/reduce_scatter | solution.py:247
  580.6 98.2 %reduce-scatter.11.cloned.1.call-done = f32[384,768]{1,0:T(8,128)} async-done(((f32[3072,768]{1,0:T(8,128)}), f32[384,768]{1,0:T(8,128)}) %reduce-scatter.11.cloned.1.call-update) | async-done | bytes 1179664 | tf_op jit(solution)/shard_map/reduce_scatter | solution.py:250
  680.9 98.1 %reduce-scatter.9.cloned.1.call-done = f32[768,384]{1,0:T(8,128)} async-done(((f32[768,3072]{1,0:T(8,128)}), f32[768,384]{1,0:T(8,128)}) %reduce-scatter.9.cloned.1.call-update) | async-done | bytes 1179664 | tf_op jit(solution)/shard_map/reduce_scatter | solution.py:249
  781.2 8.7 %fusion.113 = (f32[768]{0:T(1024)S(1)}, f32[1024,768]{1,0:T(8,128)}) fusion(bf16[768,2304]{0,1:T(8,128)(2,1)} %all-gather.5.cloned.1.call-done, bf16[1024,768]{0,1:T(8,128)(2,1)} %bitcast.218, bf16[1024,768]{0,1:T(8,128)(2,1)} %bitcast.220, bf16[1024,768]{0,1:T(8,128)(2,1)S(1)} %bitcast.216), kind=kOutput, calls=%fused_computation.168 | convolution fusion | flops 3638820096 | bytes 11406336 | tf_op jit(solution)/shard_map/te,de->td/dot_general | solution.py:238
  798.1 25.9 %all-reduce.8 = (bf16[768]{0:T(1024)(128)(2,1)S(1)}, bf16[768]{0:T(1024)(128)(2,1)S(1)}, bf16[768]{0:T(1024)(128)(2,1)S(1)}, bf16[768]{0:T(1024)(128)(2,1)S(1)}) all-reduce(f32[768]{0:T(1024)S(1)} %get-tuple-element.656, f32[768]{0:T(1024)S(1)} %get-tuple-element.744, ...), channel_id=6, replica_groups=mesh['rep'=4,'shard'=8] {'shard'}, use_global_device_ids=true, to_apply=%region_27.28.clone | all-reduce | flops 3072 | bytes 18432
  824.3 9.8 %all-reduce.10 = (bf16[96]{0:T(256)(128)(2,1)S(1)}, bf16[96]{0:T(256)(128)(2,1)S(1)}, bf16[96]{0:T(256)(128)(2,1)S(1)}, bf16[96]{0:T(256)(128)(2,1)S(1)}) all-reduce(bf16[96]{0:T(256)(128)(2,1)S(1)} %dynamic-slice.19, bf16[96]{0:T(256)(128)(2,1)S(1)} %dynamic-slice.18, ...), channel_id=1, replica_groups=mesh['rep'=4,'shard'=8] {'rep'}, use_global_device_ids=true, to_apply=%region_28.29 | all-reduce | flops 384 | bytes 1536 | tf_op jit(solution)/shard_map/psum | solution.py:261
  (283 shorter events, 233.5 us)
Async XLA Ops:
  7.2 47.2 %all-gather.5.cloned.1.call-start = ((), (), s32[]{:S(2)}) async-start(), calls=%async_computation.4 | async-start | bytes 3981312 | tf_op jit(solution)/shard_map/all_gather | solution.py:170
  7.9 188.7 %all-gather.7.cloned.1.call-start = ((), (), s32[]{:S(2)}) async-start(), calls=%async_computation.5 | async-start | bytes 1327104 | tf_op jit(solution)/shard_map/all_gather | solution.py:171
  8.7 192.2 %all-gather.9.cloned.1.call-start = ((), (), s32[]{:S(2)}) async-start(), calls=%async_computation.6 | async-start | bytes 5308416 | tf_op jit(solution)/shard_map/all_gather | solution.py:172
  9.4 202.7 %all-gather.11.cloned.1.call-start = ((), (), s32[]{:S(2)}) async-start(), calls=%async_computation.7 | async-start | bytes 5308416 | tf_op jit(solution)/shard_map/all_gather | solution.py:173
  10.0 530.3 %reduce-scatter.7.cloned.1.call-start = ((), (), s32[]{:S(2)}) async-start(), calls=%async_computation.9 | async-start | bytes 2654208 | tf_op jit(solution)/shard_map/reduce_scatter | solution.py:248
  34.6 19.7 %copy-start.48 = (f32[768]{0:T(1024)}, f32[768]{0:T(1024)S(1)}, u32[]{:S(2)}) copy-start(f32[768]{0:T(1024)S(1)} %convert_element_type.138) | copy-start | bytes 9220
  34.7 19.7 %copy-start.43 = (f32[768]{0:T(1024)}, f32[768]{0:T(1024)S(1)}, u32[]{:S(2)}) copy-start(f32[768]{0:T(1024)S(1)} %convert_element_type.137) | copy-start | bytes 9220
  38.6 15.8 %copy-start.8 = (bf16[1,1024,768]{1,2,0:T(8,128)(2,1)}, bf16[1,1024,768]{1,2,0:T(8,128)(2,1)S(1)}, u32[]{:S(2)}) copy-start(bf16[1,1024,768]{1,2,0:T(8,128)(2,1)S(1)} %copy.59) | copy-start | bytes 4718596
  38.9 22.2 %copy-start.41 = (f32[1024]{0:T(1024)}, f32[1024]{0:T(1024)S(1)}, u32[]{:S(2)}) copy-start(f32[1024]{0:T(1024)S(1)} %broadcast_multiply_fusion.7) | copy-start | bytes 12292
  39.4 21.7 %copy-start.45 = (f32[1024]{0:T(1024)}, f32[1024]{0:T(1024)S(1)}, u32[]{:S(2)}) copy-start(f32[1024]{0:T(1024)S(1)} %add_rsqrt_fusion.1) | copy-start | bytes 12292
  75.6 8.3 copy-start
  98.8 15.9 %copy-start.1 = (f32[12,512,1024]{2,1,0:T(8,128)S(1)}, f32[12,512,1024]{2,1,0:T(8,128)}, u32[]{:S(2)}) copy-start(f32[12,512,1024]{2,1,0:T(8,128)} %copy-done) | copy-start | bytes 75497472 | tf_op jit(solution)/shard_map/while
  122.4 8.1 copy-start.36
  139.5 8.5 copy-start
  162.7 15.7 %copy-start.1 = (f32[12,512,1024]{2,1,0:T(8,128)S(1)}, f32[12,512,1024]{2,1,0:T(8,128)}, u32[]{:S(2)}) copy-start(f32[12,512,1024]{2,1,0:T(8,128)} %copy-done) | copy-start | bytes 75497472 | tf_op jit(solution)/shard_map/while
  186.2 8.1 copy-start.36
  200.4 41.9 %copy-start.6 = (f32[1024,768]{0,1:T(8,128)}, f32[1024,768]{0,1:T(8,128)S(1)}, u32[]{:S(2)}) copy-start(f32[1024,768]{0,1:T(8,128)S(1)} %get-tuple-element.743) | copy-start | bytes 9437188
  200.4 41.8 %copy-start.29 = (f32[1024]{0:T(1024)}, f32[1024]{0:T(1024)S(1)}, u32[]{:S(2)}) copy-start(f32[1024]{0:T(1024)S(1)} %broadcast_multiply_fusion.6) | copy-start | bytes 12292
  200.8 41.4 %copy-start.34 = (f32[1024]{0:T(1024)}, f32[1024]{0:T(1024)S(1)}, u32[]{:S(2)}) copy-start(f32[1024]{0:T(1024)S(1)} %add_rsqrt_fusion) | copy-start | bytes 12292
  212.1 15.7 %copy-start.17 = (bf16[768,3072]{1,0:T(8,128)(2,1)S(1)}, bf16[768,3072]{1,0:T(8,128)(2,1)}, u32[]{:S(2)}) copy-start(bf16[768,3072]{1,0:T(8,128)(2,1)} %all-gather.9.cloned.1.call-done) | copy-start | bytes 14155780
  247.9 330.7 %reduce-scatter.5.cloned.1.call-start = ((), (), s32[]{:S(2)}) async-start(), calls=%async_computation.8 | async-start | bytes 7962624 | tf_op jit(solution)/shard_map/reduce_scatter | solution.py:247
  263.8 8.5 copy-start.2
  347.7 9.5 %copy-start.3 = (bf16[1024,12,64]{0,2,1:T(8,128)(2,1)S(1)}, bf16[1024,12,64]{0,2,1:T(8,128)(2,1)}, u32[]{:S(2)}) copy-start(bf16[1024,12,64]{0,2,1:T(8,128)(2,1)} %get-tuple-element.1034) | copy-start | bytes 4718596 | tf_op jit(solution)/shard_map/while
  347.7 9.5 %copy-start.14 = (bf16[2,512,12,64]{1,3,2,0:T(8,128)(2,1)S(1)}, bf16[2,512,12,64]{1,3,2,0:T(8,128)(2,1)}, u32[]{:S(2)}) copy-start(bf16[2,512,12,64]{1,3,2,0:T(8,128)(2,1)} %get-tuple-element.1008) | copy-start | bytes 4718596 | tf_op jit(solution)/shard_map/while
  376.1 8.3 copy-start.2
  460.7 9.5 %copy-start.3 = (bf16[1024,12,64]{0,2,1:T(8,128)(2,1)S(1)}, bf16[1024,12,64]{0,2,1:T(8,128)(2,1)}, u32[]{:S(2)}) copy-start(bf16[1024,12,64]{0,2,1:T(8,128)(2,1)} %get-tuple-element.1034) | copy-start | bytes 4718596 | tf_op jit(solution)/shard_map/while
  460.7 9.5 %copy-start.14 = (bf16[2,512,12,64]{1,3,2,0:T(8,128)(2,1)S(1)}, bf16[2,512,12,64]{1,3,2,0:T(8,128)(2,1)}, u32[]{:S(2)}) copy-start(bf16[2,512,12,64]{1,3,2,0:T(8,128)(2,1)} %get-tuple-element.1008) | copy-start | bytes 4718596 | tf_op jit(solution)/shard_map/while
  501.8 177.0 %reduce-scatter.11.cloned.1.call-start = ((), (), s32[]{:S(2)}) async-start(), calls=%async_computation.11 | async-start | bytes 10616832 | tf_op jit(solution)/shard_map/reduce_scatter | solution.py:250
  515.6 263.4 %reduce-scatter.9.cloned.1.call-start = ((), (), s32[]{:S(2)}) async-start(), calls=%async_computation.10 | async-start | bytes 10616832 | tf_op jit(solution)/shard_map/reduce_scatter | solution.py:249
  528.1 318.3 %all-reduce.14.cloned.1.call-start = ((), (), s32[]{:S(2)}) async-start(), calls=%async_computation.12 | async-start | bytes 3538944 | tf_op jit(solution)/shard_map/psum | solution.py:257
  542.0 239.2 %copy-start.25 = (bf16[96,8,2,512]{3,1,2,0:T(8,128)(2,1)S(1)}, bf16[96,8,2,512]{3,1,2,0:T(8,128)(2,1)}, u32[]{:S(2)}) copy-start(bf16[96,8,2,512]{3,1,2,0:T(8,128)(2,1)} %copy-done.24) | copy-start | bytes 4718596
  781.2 8.7 %copy-start.26 = (bf16[1,1024,768]{1,2,0:T(8,128)(2,1)S(1)}, bf16[1,1024,768]{1,2,0:T(8,128)(2,1)}, u32[]{:S(2)}) copy-start(bf16[1,1024,768]{1,2,0:T(8,128)(2,1)} %fusion.98) | copy-start | bytes 4718596
  (43 other events, 128.4 us)
Sparse Core Ops, SparseCore 0:
  9.7 44.6 all-gather.4
  56.0 21.5 all-gather.6
  79.2 51.2 all-gather.8
  132.0 50.4 all-gather.10
  248.0 35.7 reduce-scatter.6
  501.9 76.6 reduce-scatter.4
  580.9 97.8 reduce-scatter.10
  681.1 97.8 reduce-scatter.8
  783.0 63.2 all-reduce.13
where the time goes:
time: 867 us; the launch traced here: 860 us
  matrix products  272 us (31%)
  waiting for transfers between devices  254 us (29%)
  other arithmetic  129 us (15%)
  local copies, waits for them, and re-layouts  118 us (14%)
  blocking collectives  55 us (6%)
  loops' own time  16.4 us (2%)
  between operations  16 us (2%)
    reduce_scatter x1, waiting for transfers between devices, local(): lax.psum_scatter(grad_down, 'shard', scatter_dimension=0, tiled=True)  98.2 us
    reduce_scatter x1, waiting for transfers between devices, local(): lax.psum_scatter(grad_up, 'shard', scatter_dimension=1, tiled=True)  98.1 us
    reduce_sum x2, other arithmetic, block_step(): grad_penalty = -jnp.sum(grad_logits, axis=0)  50.5 us
    while x48, local copies, waits for them, and re-layouts  47.1 us
    unnamed x2, blocking collectives  45.1 us
    dot_general x4, matrix products, block_logits(): jnp.dot(below_mask, select, precision=highest)  41.2 us
    reduce_scatter x1, waiting for transfers between devices, local(): lax.psum_scatter(grad_qkvw, 'shard', scatter_dimension=1, tiled=True)  36.6 us
    dot_general x2, matrix products, block_step(): jnp.einsum('qhd,khd->hqk', grad_block, values, preferred_element_type=jnp...  36.5 us
  transfers between devices with their start and end apart: 9, of which 5 were waited for; matrix products, arithmetic and copies ran while one was open for 49% of the time, Pallas kernels for 0%

commit v1 on v0

v1 whole, which is shorter than its diff:
```python
import functools

import jax
import jax.numpy as jnp
from jax import lax
from jax.experimental import pallas as pl
from jax.experimental.pallas import tpu as pltpu
from jax.sharding import PartitionSpec as P

F32=jnp.float32; BF=jnp.bfloat16
NEG=-1e30
def nt(a,b):
    return lax.dot_general(a,b,(((1,),(1,)),((),())),preferred_element_type=F32)
def nn(a,b):
    return lax.dot_general(a,b,(((1,),(0,)),((),())),preferred_element_type=F32)
def tn(a,b):
    return lax.dot_general(a,b,(((0,),(0,)),((),())),preferred_element_type=F32)
def split2(x):
    hi=x.astype(BF)
    lo=(x-hi.astype(F32)).astype(BF)
    return hi,lo

def attn_fwd_kernel(BQ,G,NW,HP,unroll, nblk_ref, qkv_ref, segc_ref, segr_ref, nst_ref, o_ref, lse_ref, bias_ref, sig_ref, cs_ref):
    i=pl.program_id(0)
    D=HP*128
    @pl.when(i==0)
    def _():
        cs_ref[...]=jnp.zeros_like(cs_ref)
    row0=pl.multiple_of(i*BQ,BQ)
    nb=nblk_ref[i]
    lane=lax.broadcasted_iota(jnp.int32,(BQ,128),1)
    left=lane<64
    def variant(n):
        W=n*G
        k0=pl.multiple_of(row0+BQ-W,G)
        kw=pl.ds(k0,W)
        segq=segc_ref[pl.ds(row0,BQ),:]
        segk=segr_ref[:,kw]
        same=segq==segk
        qi=lax.broadcasted_iota(jnp.int32,(BQ,W),0)+(W-BQ)
        ki=lax.broadcasted_iota(jnp.int32,(BQ,W),1)
        allowed=same&(ki<=qi)
        chosen=same&(ki<qi)&(nst_ref[:,kw]>0)
        def qpair(p):
            return qkv_ref[pl.ds(row0,BQ),pl.ds(p,128)]*jnp.asarray(0.125,BF)
        q=qpair(0)
        k=qkv_ref[kw,pl.ds(D,128)]
        s0=nt(jnp.where(left,q,jnp.zeros_like(q)),k)
        e=jnp.exp(-jnp.abs(s0))
        sp=jnp.maximum(s0,0.0)+jnp.log1p(e)
        sg=jnp.where(s0>=0,1.0,e)/(1.0+e)
        sel=jnp.where(chosen,sp,0.0)
        sig_ref[0,:,:W]=jnp.where(chosen,sg,0.0).astype(BF)
        hi,lo=split2(sel)
        ri=lax.broadcasted_iota(jnp.int32,(BQ,BQ),0); ci=lax.broadcasted_iota(jnp.int32,(BQ,BQ),1)
        L=(ri>ci).astype(BF)
        pen=nn(L,hi)+nn(L,lo)+cs_ref[:,kw]
        cs_ref[:,kw]=cs_ref[:,kw]+jnp.sum(sel,axis=0,keepdims=True)
        bias_ref[0,:,:W]=jnp.where(allowed,-pen,NEG)
        def pair(j,lse_acc):
            off=pl.multiple_of(j*128,128)
            q=qkv_ref[pl.ds(row0,BQ),pl.ds(off,128)]*jnp.asarray(0.125,BF)
            z=jnp.zeros_like(q)
            k=qkv_ref[kw,pl.ds(D+off,128)]
            v=qkv_ref[kw,pl.ds(2*D+off,128)]
            b=bias_ref[0,:,:W]
            outs=[]
            for hh in range(2):
                qm=jnp.where(left,q,z) if hh==0 else jnp.where(left,z,q)
                s=nt(qm,k)+b
                m=jnp.max(s,axis=1,keepdims=True)
                p=jnp.exp(s-m)
                l=jnp.sum(p,axis=1,keepdims=True)
                o=nn(p.astype(BF),v)*(1.0/l)
                lse_acc=jnp.where(lane==2*j+hh,m+jnp.log(l),lse_acc)
                outs.append(o)
            o_ref[:,pl.ds(off,128)]=jnp.where(left,outs[0],outs[1]).astype(BF)
            return lse_acc
        lse_ref[...]=lax.fori_loop(0,HP,pair,jnp.zeros((BQ,128),F32),unroll=unroll)
    for n in range(1,NW+1):
        pl.when(nb==n)(functools.partial(variant,n))

def attn_fwd(qkv,segc,segr,nst,nblk,BQ=128,G=128,unroll=2):
    T,D3=qkv.shape; D=D3//3; HP=D//128
    NW=min(T//G,-(-(511+BQ)//G)) if BQ%G==0 else None
    NB=T//BQ
    whole=lambda shape: pl.BlockSpec(shape,lambda i,*_:(0,0),pipeline_mode=pl.Buffered(1))
    gs=pltpu.PrefetchScalarGridSpec(num_scalar_prefetch=1,grid=(NB,),
      in_specs=[whole((T,D3)),whole((T,1)),whole((1,T)),whole((1,T))],
      out_specs=[pl.BlockSpec((BQ,D),lambda i,*_:(i,0)),pl.BlockSpec((BQ,128),lambda i,*_:(i,0)),
        pl.BlockSpec((1,BQ,NW*G),lambda i,*_:(i,0,0)),pl.BlockSpec((1,BQ,NW*G),lambda i,*_:(i,0,0))],
      scratch_shapes=[pltpu.VMEM((1,T),F32)])
    return pl.pallas_call(functools.partial(attn_fwd_kernel,BQ,G,NW,HP,unroll),grid_spec=gs,
      out_shape=[jax.ShapeDtypeStruct((T,D),BF),jax.ShapeDtypeStruct((T,128),F32),
        jax.ShapeDtypeStruct((NB,BQ,NW*G),F32),jax.ShapeDtypeStruct((NB,BQ,NW*G),BF)],
      compiler_params=pltpu.CompilerParams(vmem_limit_bytes=40<<20),name="attn_fwd")(nblk,qkv,segc,segr,nst)

def attn_bwd_kernel(BQ,G,NW,HP,unroll,NB, nblk_ref, qkv_ref, do_ref, o_ref, lse_ref, bias_ref, sig_ref, out_ref, dk_ref, dv_ref, gp_ref, ls_ref):
    step=pl.program_id(0)
    i=NB-1-step
    D=HP*128
    @pl.when(step==0)
    def _():
        dk_ref[...]=jnp.zeros_like(dk_ref)
        dv_ref[...]=jnp.zeros_like(dv_ref)
        ls_ref[...]=jnp.zeros_like(ls_ref)
    row0=pl.multiple_of(i*BQ,BQ)
    nb=nblk_ref[i]
    lane=lax.broadcasted_iota(jnp.int32,(BQ,128),1)
    left=lane<64
    def variant(n):
        W=n*G
        k0=pl.multiple_of(row0+BQ-W,G)
        kw=pl.ds(k0,W)
        gp_ref[:,:W]=jnp.zeros((BQ,W),F32)
        ones=jnp.ones((W,128),BF)
        lse=lse_ref[...]
        def work(j,first):
            off=pl.multiple_of(j*128,128)
            q=qkv_ref[pl.ds(row0,BQ),pl.ds(off,128)]*jnp.asarray(0.125,BF)
            k=qkv_ref[kw,pl.ds(D+off,128)]
            v=qkv_ref[kw,pl.ds(2*D+off,128)]
            do=do_ref[:,pl.ds(off,128)]
            z=jnp.zeros_like(q)
            b=bias_ref[0,:,:W]
            prod=do.astype(F32)*o_ref[:,pl.ds(off,128)].astype(F32)
            qs=[jnp.where(left,q,z),jnp.where(left,z,q)]
            dos=[jnp.where(left,do,z),jnp.where(left,z,do)]
            ps=[];dss=[]
            for hh in range(2):
                lh=jnp.sum(jnp.where(lane==2*j+hh,lse,0.0),axis=1,keepdims=True)
                delta=jnp.sum(jnp.where(left,prod,0.0) if hh==0 else jnp.where(left,0.0,prod),axis=1,keepdims=True)
                s=nt(qs[hh],k)
                p=jnp.exp(s+b-lh)
                dp=nt(dos[hh],v)
                ps.append(p); dss.append(p*(dp-delta))
            if not first:
                gp_ref[:,:W]=gp_ref[:,:W]+(dss[0]+dss[1])
            else:
                gp=gp_ref[:,:W]+(dss[0]+dss[1])
                hi,lo=split2(gp)
                ri=lax.broadcasted_iota(jnp.int32,(BQ,BQ),0); ci=lax.broadcasted_iota(jnp.int32,(BQ,BQ),1)
                U=(ci>ri).astype(BF)
                gsel=nn(U,hi)+nn(U,lo)+ls_ref[:,kw]
                ls_ref[:,kw]=ls_ref[:,kw]+jnp.sum(gp,axis=0,keepdims=True)
                dss[0]=dss[0]-gsel*sig_ref[0,:,:W].astype(F32)
            dsb=[x.astype(BF) for x in dss]
            pb=[x.astype(BF) for x in ps]
            dq=jnp.where(left,nn(dsb[0],k),nn(dsb[1],k))*0.125
            out_ref[pl.ds(row0,BQ),pl.ds(off,128)]=dq.astype(BF)
            dk_ref[kw,pl.ds(off,128)]+=tn(dsb[0],qs[0])+tn(dsb[1],qs[1])
            dv_ref[kw,pl.ds(off,128)]+=tn(pb[0],dos[0])+tn(pb[1],dos[1])
        def body(j,c):
            work(j,False)
            return c
        lax.fori_loop(1,HP,body,0,unroll=unroll)
        work(0,True)
    for n in range(1,NW+1):
        pl.when(nb==n)(functools.partial(variant,n))
    @pl.when(step==NB-1)
    def _():
        out_ref[:,D:2*D]=dk_ref[...].astype(BF)
        out_ref[:,2*D:]=dv_ref[...].astype(BF)

def attn_bwd(qkv,do,o,lse,bias,sig,nblk,BQ=128,G=128,unroll=1):
    T,D3=qkv.shape; D=D3//3; HP=D//128
    NW=bias.shape[2]//G
    NB=T//BQ
    whole=lambda shape: pl.BlockSpec(shape,lambda i,*_:(0,0),pipeline_mode=pl.Buffered(1))
    rb=lambda w: pl.BlockSpec((BQ,w),lambda i,*_:(NB-1-i,0))
    r3=pl.BlockSpec((1,BQ,NW*G),lambda i,*_:(NB-1-i,0,0))
    gs=pltpu.PrefetchScalarGridSpec(num_scalar_prefetch=1,grid=(NB,),
      in_specs=[whole((T,D3)),rb(D),rb(D),rb(128),r3,r3],
      out_specs=whole((T,D3)),
      scratch_shapes=[pltpu.VMEM((T,D),F32),pltpu.VMEM((T,D),F32),pltpu.VMEM((BQ,NW*G),F32),pltpu.VMEM((1,T),F32)])
    return pl.pallas_call(functools.partial(attn_bwd_kernel,BQ,G,NW,HP,unroll,NB),grid_spec=gs,
      out_shape=jax.ShapeDtypeStruct((T,D3),BF),
      compiler_params=pltpu.CompilerParams(vmem_limit_bytes=50<<20),name="attn_bwd")(nblk,qkv,do,o,lse,bias,sig)

def prep(seg,BQ=128,G=128):
    T=seg.shape[0]
    NB=T//BQ
    at=seg[::BQ]
    first=jnp.sum((seg[None,:]<at[:,None]).astype(jnp.int32),axis=1)
    ends=(jnp.arange(NB,dtype=jnp.int32)+1)*BQ
    nblk=(ends-(first//G)*G)//G
    starts=jnp.concatenate([jnp.ones((1,),bool),seg[1:]!=seg[:-1]])
    nst=jnp.logical_not(starts).astype(jnp.int32)[None,:]
    return seg[:,None],seg[None,:],nst,nblk

EPS=1e-5
GC=0.7978845608028654; GA=0.044715
def rowmean(x): return jnp.mean(x,axis=-1,keepdims=True)
def ln_unit(x):
    m=rowmean(x); c=x-m; v=rowmean(c*c); r=lax.rsqrt(v+EPS)
    return c*r, r

def qkv_kernel(tok_ref,w_ref,vec_ref,n_ref,o_ref):
    u,_=ln_unit(tok_ref[...].astype(F32))
    n=(u*vec_ref[0:1,:]+vec_ref[1:2,:]).astype(BF)
    n_ref[...]=n
    o_ref[...]=nt(n,w_ref[...]).astype(BF)
def qkv_proj(tok,wT,vec,R=256):
    T,D=tok.shape; E=wT.shape[0]
    c=lambda s: pl.BlockSpec(s,lambda i:(0,0),pipeline_mode=pl.Buffered(1))
    return pl.pallas_call(qkv_kernel,grid=(T//R,),in_specs=[pl.BlockSpec((R,D),lambda i:(i,0)),c((E,D)),c(vec.shape)],
      out_specs=[pl.BlockSpec((R,D),lambda i:(i,0)),pl.BlockSpec((R,E),lambda i:(i,0))],
      out_shape=[jax.ShapeDtypeStruct((T,D),BF),jax.ShapeDtypeStruct((T,E),BF)],
      compiler_params=pltpu.CompilerParams(vmem_limit_bytes=40<<20),name="qkv_proj")(tok,wT,vec)

def mlp_kernel(NR,NC,C,R,tok_ref,att_ref,cot_ref,ow_ref,up_ref,dn_ref,vec_ref,
    out_ref,gres_ref,gatt_ref,gdn_ref,gup_ref,gow_ref,vg_ref, act_s,gh_s,n2_s,gb_s):
    i=pl.program_id(0)
    @pl.when(i<NR)
    def _():
        rows=pl.ds(pl.multiple_of(i*R,R),R)
        gain=vec_ref[2:3,:]; shift=vec_ref[3:4,:]
        res=tok_ref[rows,:].astype(F32)+nn(att_ref[rows,:],ow_ref[...])
        u,rstd=ln_unit(res)
        n2=(u*gain+shift).astype(BF)
        n2_s[rows,:]=n2
        cot=cot_ref[rows,:]
        out_acc=res
        g_acc=jnp.zeros_like(res)
        for c in range(NC):
            cs=slice(c*C,(c+1)*C)
            h=nt(n2,up_ref[cs,:])
            h2=h*h
            t=jnp.tanh(h*(GC+GC*GA*h2))
            half=0.5*(1.0+t)
            act=(h*half).astype(BF)
            act_s[rows,cs]=act
            ga=nt(cot,dn_ref[cs,:])
            dg=half+(0.5*h)*(1.0-t*t)*(GC+3.0*GC*GA*h2)
            gh=(ga*dg).astype(BF)
            gh_s[rows,cs]=gh
            out_acc=out_acc+nn(act,dn_ref[cs,:])
            g_acc=g_acc+nn(gh,up_ref[cs,:])
        out_ref[...]=out_acc.astype(BF)
        vgain=jnp.sum(g_acc*u,axis=0,keepdims=True); vshift=jnp.sum(g_acc,axis=0,keepdims=True)
        @pl.when(i==0)
        def _():
            vg_ref[...]=jnp.zeros_like(vg_ref)
        vg_ref[0:1,:]+=vgain
        vg_ref[1:2,:]+=vshift
        g=g_acc*gain
        gr=cot.astype(F32)+rstd*(g-rowmean(g)-u*rowmean(g*u))
        gres_ref[...]=gr
        gb=gr.astype(BF)
        gb_s[rows,:]=gb
        gatt_ref[...]=nt(gb,ow_ref[...]).astype(BF)
    @pl.when(i>=NR)
    def _():
        j=i-NR
        cs=pl.ds(pl.multiple_of(j*C2(gdn_ref),C2(gdn_ref)),C2(gdn_ref))
        gdn_ref[...]=tn(act_s[:,cs],cot_ref[...]).astype(BF)
        gup_ref[...]=tn(gh_s[:,cs],n2_s[...]).astype(BF)
    @pl.when(i==NR)
    def _():
        gow_ref[...]=tn(att_ref[...],gb_s[...]).astype(BF)
def C2(ref): return ref.shape[0]
def mlp(tok,att,cot,ow,upT,dn,vec,R=256,C=768,WC=384):
    T,D=tok.shape; F=upT.shape[0]; NR=T//R; NW=F//WC
    c=lambda s: pl.BlockSpec(s,lambda i:(0,0),pipeline_mode=pl.Buffered(1))
    rb=lambda w: pl.BlockSpec((R,w),lambda i:(jnp.minimum(i,NR-1),0))
    wb=pl.BlockSpec((WC,D),lambda i:(jnp.maximum(i-NR,0),0))
    return pl.pallas_call(functools.partial(mlp_kernel,NR,F//C,C,R),grid=(NR+NW,),
      in_specs=[c((T,D)),c((T,D)),c((T,D)),c((D,D)),c((F,D)),c((F,D)),c(vec.shape)],
      out_specs=[rb(D),rb(D),rb(D),wb,wb,c((D,D)),c((8,D))],
      out_shape=[jax.ShapeDtypeStruct((T,D),BF),jax.ShapeDtypeStruct((T,D),F32),jax.ShapeDtypeStruct((T,D),BF),
        jax.ShapeDtypeStruct((F,D),BF),jax.ShapeDtypeStruct((F,D),BF),jax.ShapeDtypeStruct((D,D),BF),jax.ShapeDtypeStruct((8,D),F32)],
      scratch_shapes=[pltpu.VMEM((T,F),BF),pltpu.VMEM((T,F),BF),pltpu.VMEM((T,D),BF),pltpu.VMEM((T,D),BF)],
      compiler_params=pltpu.CompilerParams(vmem_limit_bytes=58<<20),name="mlp")(tok,att,cot,ow,upT,dn,vec)

def wg_kernel(gp_ref,n_ref,o_ref):
    o_ref[...]=tn(gp_ref[...],n_ref[...]).astype(BF)
def qkv_wgrad(gp,n1,WC=384):
    T,E=gp.shape; D=n1.shape[1]
    return pl.pallas_call(wg_kernel,grid=(E//WC,),in_specs=[pl.BlockSpec((T,WC),lambda i:(0,i)),pl.BlockSpec((T,D),lambda i:(0,0),pipeline_mode=pl.Buffered(1))],
      out_specs=pl.BlockSpec((WC,D),lambda i:(i,0)),out_shape=jax.ShapeDtypeStruct((E,D),BF),
      compiler_params=pltpu.CompilerParams(vmem_limit_bytes=40<<20),name="qkv_wgrad")(gp,n1)
def dg_kernel(gp_ref,w_ref,tok_ref,gres_ref,vec_ref,o_ref,vg_ref):
    i=pl.program_id(0)
    gn=nn(gp_ref[...],w_ref[...])
    u,rstd=ln_unit(tok_ref[...].astype(F32))
    @pl.when(i==0)
    def _():
        vg_ref[...]=jnp.zeros_like(vg_ref)
    vg_ref[0:1,:]+=jnp.sum(gn*u,axis=0,keepdims=True)
    vg_ref[1:2,:]+=jnp.sum(gn,axis=0,keepdims=True)
    g=gn*vec_ref[0:1,:]
    o_ref[...]=(gres_ref[...]+rstd*(g-rowmean(g)-u*rowmean(g*u))).astype(BF)
def qkv_dgrad(gp,wT,tok,gres,vec,R=256):
    T,E=gp.shape; D=tok.shape[1]
    c=lambda s: pl.BlockSpec(s,lambda i:(0,0),pipeline_mode=pl.Buffered(1))
    rb=lambda w: pl.BlockSpec((R,w),lambda i:(i,0))
    return pl.pallas_call(dg_kernel,grid=(T//R,),in_specs=[rb(E),c((E,D)),rb(D),rb(D),c(vec.shape)],out_specs=[rb(D),c((8,D))],
      out_shape=[jax.ShapeDtypeStruct((T,D),BF),jax.ShapeDtypeStruct((8,D),F32)],
      compiler_params=pltpu.CompilerParams(vmem_limit_bytes=40<<20),name="qkv_dgrad")(gp,wT,tok,gres,vec)


def gather(x):
    return lax.all_gather(x, "shard", axis=0, tiled=True)


def reduce_shard(g):
    part = lax.psum_scatter(g, "shard", scatter_dimension=0, tiled=True)
    return lax.psum(part, "rep").astype(F32)


def local(tokens, segment_ids, qkv_weight, out_weight, up_weight, down_weight,
          norm1_gain, norm1_shift, norm2_gain, norm2_shift, cotangent):
    tok = tokens[0]
    cot = cotangent[0]
    seg = segment_ids[0]
    model = tok.shape[1]
    shards = lax.axis_size("shard")
    width = qkv_weight.shape[1]
    vec_part = jnp.stack([norm1_gain, norm1_shift, norm2_gain, norm2_shift])
    vec_rows = jnp.zeros((8, model), BF).at[:4, : vec_part.shape[1]].set(vec_part)
    first = gather(jnp.concatenate([qkv_weight.T, vec_rows], axis=0)).reshape(shards, width + 8, model)
    qkv_t = first[:, :width].reshape(shards * width, model)
    vec = first[:, width:, : vec_part.shape[1]].transpose(1, 0, 2).reshape(8, model).astype(F32)
    out_full = gather(out_weight)
    up_t = gather(up_weight.T)
    down_full = gather(down_weight)
    segc, segr, nst, nblk = prep(seg)
    normed, projected = qkv_proj(tok, qkv_t, vec)
    attended, lse, bias, sig = attn_fwd(projected, segc, segr, nst, nblk, unroll=6)
    output, gres, gatt, gdn, gup, gow, vec2 = mlp(tok, attended, cot, out_full, up_t, down_full, vec)
    gproj = attn_bwd(projected, gatt, attended, lse, bias, sig, nblk, unroll=5)
    gqkv = qkv_wgrad(gproj, normed)
    tgrad, vec1 = qkv_dgrad(gproj, qkv_t, tok, gres, vec)
    down_grad = reduce_shard(gdn)
    up_grad = reduce_shard(gup).T
    out_grad = reduce_shard(gow)
    qkv_grad = reduce_shard(gqkv).T
    vec_all = lax.psum(jnp.concatenate([vec1[:2], vec2[:2]], axis=0), ("rep", "shard"))
    piece = norm1_gain.shape[0]
    mine = lax.dynamic_slice_in_dim(vec_all, lax.axis_index("shard") * piece, piece, 1)
    return (output[None], tgrad[None], qkv_grad, out_grad, up_grad, down_grad,
            mine[0], mine[1], mine[2], mine[3])


def solution(mesh):
    seq = P(("rep", "shard"), None, None)
    cols, rows, vecs = P(None, "shard"), P("shard", None), P("shard")
    return jax.shard_map(
        local,
        mesh=mesh,
        in_specs=(seq, P(("rep", "shard"), None), cols, rows, cols, rows, vecs, vecs, vecs, vecs, seq),
        out_specs=(seq, seq, cols, rows, cols, rows, vecs, vecs, vecs, vecs),
        check_vma=False,
    )
```

time: 867 us -> 520 us (0.60)
  matrix products: 272 us -> 0 us
  other arithmetic: 129 us -> 7.53 us
  Pallas kernels: 0 us -> 117 us
  local copies, waits for them, and re-layouts: 118 us -> 33.3 us
  waiting for transfers between devices: 254 us -> 300 us
  blocking collectives: 55 us -> 38.2 us
  loops' own time: 16.4 us -> 0 us
    dot_general x32 -> x0, matrix products: 272 us -> none  [the longest x4 41.2 us: block_logits(): jnp.dot(below_mask, select, precision=highest)]
    pallas_call x0 -> x6, Pallas kernels: none -> 117 us  [the longest x1 49.9 us: mlp(): pl.pallas_call(functools.partial(mlp_kernel, NR, F // C, C, R), grid=(NR...]
    all_gather x4, waiting for transfers between devices: 13.3 us -> 129 us  [gather(): return lax.all_gather(x, 'shard', axis=0, tiled=True)]
    reduce_scatter x4, waiting for transfers between devices: 233 us -> 153 us  [reduce_shard(): part = lax.psum_scatter(g, 'shard', scatter_dimension=0, tiled=True)]
    reduce_sum x11 -> x1, other arithmetic: 77 us -> 0.2 us  [prep(): first = jnp.sum((seg[None, :] < at[:, None]).astype(jnp.int32), axis=1)]
    while x48 -> x0, local copies, waits for them, and re-layouts: 47.1 us -> none
    unnamed x2 -> x0, blocking collectives: 45.1 us -> none
    psum x1, blocking collectives: 9.83 us -> 38.2 us  [local(): lax.psum(jnp.concatenate([vec1[:2], vec2[:2]], axis=0), ('rep', 'shard'))]
  transfers between devices with their start and end apart: 9 -> 9, of which waited for: 5 -> 7; matrix products, arithmetic and copies ran while one was open for 49% -> 2% of each run, Pallas kernels for 0% -> 13%
where the time goes in v1:
time: 520 us; the launch traced here: 510 us
  waiting for transfers between devices  300 us (58%)
  Pallas kernels  117 us (22%)
  blocking collectives  38.2 us (7%)
  local copies, waits for them, and re-layouts  33.3 us (6%)
  between operations  14.5 us (3%)
  other arithmetic  7.53 us (1%)
    reduce_scatter x4, waiting for transfers between devices, reduce_shard(): part = lax.psum_scatter(g, 'shard', scatter_dimension=0, tiled=True)  153 us
    all_gather x4, waiting for transfers between devices, gather(): return lax.all_gather(x, 'shard', axis=0, tiled=True)  129 us
    pallas_call x1, Pallas kernels, mlp(): pl.pallas_call(functools.partial(mlp_kernel, NR, F // C, C, R), grid=(NR...  49.9 us
    psum x1, blocking collectives, local(): lax.psum(jnp.concatenate([vec1[:2], vec2[:2]], axis=0), ('rep', 'shard'))  38.2 us
    pallas_call x1, Pallas kernels, attn_bwd(): pl.pallas_call(functools.partial(attn_bwd_kernel, BQ, G, NW, HP, unroll,...  28.4 us
    unnamed x50, local copies, waits for them, and re-layouts  26.5 us
    pallas_call x1, Pallas kernels, attn_fwd(): pl.pallas_call(functools.partial(attn_fwd_kernel, BQ, G, NW, HP, unroll),...  20.8 us
    psum x1, waiting for transfers between devices, reduce_shard(): return lax.psum(part, 'rep').astype(F32)  14.7 us
  transfers between devices with their start and end apart: 9, of which 7 were waited for; matrix products, arithmetic and copies ran while one was open for 2% of the time, Pallas kernels for 13%

profile of v1, /device:TPU:0, one launch (start us, length us, event | category | flops | bytes accessed | tf_op | source)
XLA Modules:
  0.0 510.3 jit_solution(16044201792090155897)
XLA Ops:
  8.0 1.8 pad_maximum_fusion
  13.9 41.4 %all-gather.5.cloned.1.call-done = bf16[2368,768]{1,0:T(8,128)(2,1)} async-done(((bf16[296,768]{1,0:T(8,128)(2,1)}), bf16[2368,768]{1,0:T(8,128)(2,1)}) %all-gather.5.cloned.1.call-update) | async-done | bytes 3637264 | tf_op jit(solution)/shard_map/all_gather | solution.py:303
  56.0 2.2 slice.66
  58.9 1.4 reshape.91.vec_ref
  60.3 1.4 copy-done.4
  62.5 5.3 %qkv_proj.1 = (bf16[1024,768]{1,0:T(8,128)(2,1)S(1)}, bf16[1024,2304]{1,0:T(8,128)(2,1)S(1)}) custom-call(bf16[1024,768]{1,0:T(8,128)(2,1)S(1)} %bitcast.29, bf16[2304,768]{1,0:T(8,128)(2,1)S(1)} %bitcast.26, f32[8,768]{1,0:T(8,128)S(1)} %copy-done.17), custom_call_target="tpu_custom_call" | custom-call | tf_op jit(solution)/shard_map/qkv_proj/pallas_call | solution.py:206
  67.8 1.1 copy-done.10
  68.9 20.8 %attn_fwd.1 = (bf16[1024,768]{1,0:T(8,128)(2,1)S(1)}, f32[1024,128]{1,0:T(8,128)S(1)}, f32[8,128,640]{2,1,0:T(8,128)S(1)}, bf16[8,128,640]{2,1,0:T(8,128)(2,1)S(1)}) custom-call(s32[8]{0:T(128)S(1)} %and_select_fusion.nblk_ref, bf16[1024,2304]{1,0:T(8,128)(2,1)S(1)} %get-tuple-element.37.qkv_ref, s32[1024,1]{1,0:T(8,128)S(1)} %copy-done.9, ...), custom_call_target="tpu_custom_call" | custom-call | tf_op jit(solution)/shard_map/attn_fwd/pallas_call | solution.py:93
  89.7 2.1 copy-done.2
  91.8 1.1 copy-done.6
  92.9 1.5 copy-done.8
  94.5 1.1 copy-done.13
  96.3 35.8 %all-gather.9.cloned.1.call-done.up_ref = bf16[3072,768]{1,0:T(8,128)(2,1)} async-done(((bf16[384,768]{1,0:T(8,128)(2,1)}), bf16[3072,768]{1,0:T(8,128)(2,1)}) %all-gather.9.cloned.1.call-update) | async-done | bytes 4718608 | tf_op jit(solution)/shard_map/all_gather | solution.py:303
  132.1 52.0 %all-gather.11.cloned.1.call-done.dn_ref = bf16[3072,768]{1,0:T(8,128)(2,1)} async-done(((bf16[384,768]{1,0:T(8,128)(2,1)}), bf16[3072,768]{1,0:T(8,128)(2,1)}) %all-gather.11.cloned.1.call-update) | async-done | bytes 4718608 | tf_op jit(solution)/shard_map/all_gather | solution.py:303
  184.1 49.9 %mlp.1 = (bf16[1024,768]{1,0:T(8,128)(2,1)}, f32[1024,768]{1,0:T(8,128)}, bf16[1024,768]{1,0:T(8,128)(2,1)}, bf16[3072,768]{1,0:T(8,128)(2,1)}, bf16[3072,768]{1...) custom-call(bf16[1024,768]{1,0:T(8,128)(2,1)} %bitcast.28, bf16[1024,768]{1,0:T(8,128)(2,1)} %copy-done.6, ...), custom_call_target="tpu_custom_call" | custom-call | tf_op jit(solution)/shard_map/mlp/pallas_call | solution.py:267
  234.1 1.4 copy-done.12
  235.5 1.3 copy-done.14
  237.9 28.4 %attn_bwd.1.gp_ref = bf16[1024,2304]{1,0:T(8,128)(2,1)} custom-call(s32[8]{0:T(128)S(1)} %and_select_fusion.nblk_ref, bf16[1024,2304]{1,0:T(8,128)(2,1)} %copy-done.2, bf16[1024,768]{1,0:T(8,128)(2,1)S(1)} %copy-done.12, bf16[1024,768]{1,0:T(8,128)(2,1)} %copy-done.6, f32[1024,128]{1,0:T(8,128)S(1)} %copy-done.16, f32[8,128,640]{2,1,0:T(8,128)} %copy-done.8, ...), custom_call_target="tpu_custom_call" | custom-call | tf_op jit(solution)/shard_map/attn_bwd/pallas_call | solution.py:176
  266.3 2.3 copy-done
  268.6 5.5 %qkv_wgrad.1 = bf16[2304,768]{1,0:T(8,128)(2,1)S(1)} custom-call(bf16[1024,2304]{1,0:T(8,128)(2,1)S(1)} %copy-done, bf16[1024,768]{1,0:T(8,128)(2,1)S(1)} %copy-done.11), custom_call_target="tpu_custom_call" | custom-call | tf_op jit(solution)/shard_map/qkv_wgrad/pallas_call | solution.py:279
  274.1 1.7 copy-done.3
  277.4 41.3 %reduce-scatter.5.cloned.1.call-done = bf16[288,768]{1,0:T(8,128)(2,1)} async-done(((bf16[2304,768]{1,0:T(8,128)(2,1)}), bf16[288,768]{1,0:T(8,128)(2,1)}) %reduce-scatter.5.cloned.1.call-update) | async-done | bytes 442384 | tf_op jit(solution)/shard_map/reduce_scatter | solution.py:307
  318.7 55.9 %reduce-scatter.9.cloned.1.call-done = bf16[384,768]{1,0:T(8,128)(2,1)} async-done(((bf16[3072,768]{1,0:T(8,128)(2,1)}), bf16[384,768]{1,0:T(8,128)(2,1)}) %reduce-scatter.9.cloned.1.call-update) | async-done | bytes 589840 | tf_op jit(solution)/shard_map/reduce_scatter | solution.py:307
  374.6 55.8 %reduce-scatter.11.cloned.1.call-done = bf16[384,768]{1,0:T(8,128)(2,1)} async-done(((bf16[3072,768]{1,0:T(8,128)(2,1)}), bf16[384,768]{1,0:T(8,128)(2,1)}) %reduce-scatter.11.cloned.1.call-update) | async-done | bytes 589840 | tf_op jit(solution)/shard_map/reduce_scatter | solution.py:307
  430.4 2.3 copy-done.1
  432.8 1.4 copy-done.5
  434.2 1.9 copy-done.7
  436.8 7.1 %qkv_dgrad.1 = (bf16[1024,768]{1,0:T(8,128)(2,1)}, f32[8,768]{1,0:T(8,128)S(1)}) custom-call(bf16[1024,2304]{1,0:T(8,128)(2,1)S(1)} %copy-done.1, bf16[2304,768]{1,0:T(8,128)(2,1)S(1)} %bitcast.27, bf16[1024,768]{1,0:T(8,128)(2,1)S(1)} %bitcast.30, f32[1024,768]{1,0:T(8,128)S(1)} %copy-done.7, f32[8,768]{1,0:T(8,128)S(1)} %copy-done.18), custom_call_target="tpu_custom_call" | custom-call | tf_op jit(solution)/shard_map/qkv_dgrad/pallas_call | solution.py:297
  444.7 38.2 %psum.39 = f32[4,768]{1,0:T(4,128)S(1)} all-reduce(f32[4,768]{1,0:T(4,128)S(1)} %pad_maximum_fusion.1), channel_id=1, replica_groups=mesh['rep'=4,'shard'=8] {'rep','shard'}, use_global_device_ids=true, to_apply=%region_9.10 | all-reduce | flops 3072 | bytes 24576 | tf_op jit(solution)/shard_map/psum | solution.py:338
  483.4 14.7 %all-reduce.4.cloned.1.call-done = (bf16[768,384]{0,1:T(8,128)(2,1)}, bf16[768,288]{0,1:T(8,128)(2,1)}, bf16[96,768]{1,0:T(8,128)(2,1)}, bf16[384,768]{1,0:T(8,128)(2,1)}) async-done(((bf16[768,384]{0,1:T(8,128)(2,1)}, bf16[768,288]{0,1:T(8,128)(2,1)}, bf16[96,768]{1,0:T(8,128)(2,1)}, bf16[384,768]{1,0:T(8,128)(2,1)}), (bf16[768,384]{0,1:T(8,128)(2,1)}, bf16[768,288]{0,1:T(8,128)(2,1)}, ...) | async-done | bytes 1769488 | tf_op jit(solution)/shard_map/psum | solution.py:308
  498.2 2.2 convert_element_type.34
  500.4 1.3 copy.31
  (72 shorter events, 14.2 us)
Async XLA Ops:
  7.2 3.5 copy-start.21
  7.2 48.1 %all-gather.5.cloned.1.call-start = ((), (), s32[]{:S(2)}) async-start(), calls=%async_computation.4 | async-start | bytes 4091904 | tf_op jit(solution)/shard_map/all_gather | solution.py:303
  9.8 2.6 copy-start.19
  9.8 86.5 %all-gather.7.cloned.1.call-start = ((), (), s32[]{:S(2)}) async-start(), calls=%async_computation.5 | async-start | bytes 1327104 | tf_op jit(solution)/shard_map/all_gather | solution.py:303
  10.6 121.5 %all-gather.9.cloned.1.call-start = ((), (), s32[]{:S(2)}) async-start(), calls=%async_computation.6 | async-start | bytes 5308416 | tf_op jit(solution)/shard_map/all_gather | solution.py:303
  11.7 172.4 %all-gather.11.cloned.1.call-start = ((), (), s32[]{:S(2)}) async-start(), calls=%async_computation.7 | async-start | bytes 5308416 | tf_op jit(solution)/shard_map/all_gather | solution.py:303
  12.3 265.1 %reduce-scatter.7.cloned.1.call-start = ((), (), s32[]{:S(2)}) async-start(), calls=%async_computation.9 | async-start | bytes 1327104 | tf_op jit(solution)/shard_map/reduce_scatter | solution.py:307
  60.3 1.4 copy-start.4
  61.7 0.7 copy-start.17
  62.5 6.4 %copy-start.9 = (s32[1024,1]{1,0:T(8,128)S(1)}, s32[1024,1]{1,0:T(8,128)}, u32[]{:S(2)}) copy-start(s32[1024,1]{1,0:T(8,128)} %copy.29.segc_ref) | copy-start | bytes 12292
  67.8 1.1 copy-start.10
  89.7 2.1 copy-start.2
  91.8 1.1 copy-start.6
  92.9 1.5 copy-start.8
  94.5 1.1 copy-start.13
  95.5 0.8 copy-start.15
  234.0 84.7 %reduce-scatter.5.cloned.1.call-start = ((), (), s32[]{:S(2)}) async-start(), calls=%async_computation.8 | async-start | bytes 3981312 | tf_op jit(solution)/shard_map/reduce_scatter | solution.py:307
  234.1 1.4 copy-start.12
  235.5 1.3 copy-start.14
  236.8 1.0 copy-start.16
  237.9 28.4 %copy-start.11 = (bf16[1024,768]{1,0:T(8,128)(2,1)S(1)}, bf16[1024,768]{1,0:T(8,128)(2,1)}, u32[]{:S(2)}) copy-start(bf16[1024,768]{1,0:T(8,128)(2,1)} %copy-done.10) | copy-start | bytes 4718596
  266.2 2.3 copy-start
  274.1 1.8 copy-start.3
  275.9 98.8 %reduce-scatter.9.cloned.1.call-start = ((), (), s32[]{:S(2)}) async-start(), calls=%async_computation.10 | async-start | bytes 5308416 | tf_op jit(solution)/shard_map/reduce_scatter | solution.py:307
  276.6 153.8 %reduce-scatter.11.cloned.1.call-start = ((), (), s32[]{:S(2)}) async-start(), calls=%async_computation.11 | async-start | bytes 5308416 | tf_op jit(solution)/shard_map/reduce_scatter | solution.py:307
  277.4 220.8 %all-reduce.4.cloned.1.call-start = ((), (), s32[]{:S(2)}) async-start(), calls=%async_computation.12 | async-start | bytes 3538944 | tf_op jit(solution)/shard_map/psum | solution.py:308
  430.4 2.3 copy-start.1
  432.8 1.4 copy-start.5
  434.2 1.9 copy-start.7
  498.2 2.2 copy-start.20
  498.2 3.5 copy-start.22
  500.4 2.2 copy-start.23
  (1 other events, 0.7 us)
Sparse Core Ops, SparseCore 0:
  10.2 45.0 all-gather.4
  56.9 21.5 all-gather.6
  80.8 51.2 all-gather.8
  133.6 50.4 all-gather.10
  234.2 31.4 reduce-scatter.6
  276.0 42.6 reduce-scatter.4
  321.1 53.4 reduce-scatter.8
  377.0 53.3 reduce-scatter.10
  434.3 63.8 all-reduce.3

commit v2 on v1

--- a/solution.py
+++ b/solution.py
@@ -7,7 +7,8 @@
 from jax.experimental.pallas import tpu as pltpu
 from jax.sharding import PartitionSpec as P
 
-F32=jnp.float32; BF=jnp.bfloat16
+F32 = jnp.float32
+BF = jnp.bfloat16
 NEG=-1e30
 def nt(a,b):
     return lax.dot_general(a,b,(((1,),(1,)),((),())),preferred_element_type=F32)
@@ -298,14 +299,228 @@
       out_shape=[jax.ShapeDtypeStruct((T,D),BF),jax.ShapeDtypeStruct((8,D),F32)],
       compiler_params=pltpu.CompilerParams(vmem_limit_bytes=40<<20),name="qkv_dgrad")(gp,wT,tok,gres,vec)
 
+MESH=pl.DeviceIdType.MESH
+
+def place():
+    r=lax.axis_index("rep"); s=lax.axis_index("shard")
+    y=r//2; x=r%2; z=s//2; c=s%2
+    return dict(r=r,s=s,y=y,x=x,z=z,c=c,rx=y*2+(1-x),ry=(1-y)*2+x,rd=(1-y)*2+(1-x),mate=z*2+(1-c))
+def zpeer(p,dz):
+    return (p["z"]+dz)%4
+def greet(p):
+    bar=pltpu.get_barrier_semaphore()
+    for dev in ((p["r"],p["mate"]),(p["rx"],p["s"]),(p["ry"],p["s"]))+tuple((p["r"],zpeer(p,dz)*2+p["c"]) for dz in (1,2,3)):
+        pl.semaphore_signal(bar,inc=1,device_id=dev,device_id_type=MESH)
+    pl.semaphore_wait(bar,6)
+def rcopy(src,dst,ss,rs,dev):
+    return pltpu.make_async_remote_copy(src_ref=src,dst_ref=dst,send_sem=ss,recv_sem=rs,device_id=dev,device_id_type=MESH)
+
+def gather_kernel(q_ref,o_ref,u_ref,d_ref,v_ref,qf,of,uf,df,vf,vz,vp,vm,lsem,c0s,c0r,ss,rs,vs,vr):
+    p=place()
+    greet(p)
+    r,s,c,z=p["r"],p["s"],p["c"],p["z"]
+    mate=(r,p["mate"]); xm=(p["rx"],s); ym=(p["ry"],s)
+    sets=((q_ref,qf),(o_ref,of),(u_ref,uf),(d_ref,df))
+    done=[]
+    def go(cp):
+        cp.start(); done.append(cp); return cp
+    locs=[]
+    for w,(a,f) in enumerate(sets):
+        cp=pltpu.make_async_copy(a,f.at[s],lsem.at[w]); cp.start(); locs.append(cp)
+    H=q_ref.shape[1]//2
+    vcs=[go(rcopy(v_ref,vz.at[dz-1],vs.at[dz-1],vr.at[dz-1],(r,zpeer(p,dz)*2+c))) for dz in (1,2,3)]
+    def zsend(w):
+        a,f=sets[w]; Q=a.shape[0]//4
+        rows=pl.ds(pl.multiple_of(r*Q,8),Q)
+        return [go(rcopy(a.at[rows],f.at[s,rows],ss.at[w,0,dz-1],rs.at[w,0,dz-1],(r,zpeer(p,dz)*2+c))) for dz in (1,2,3)]
+    def core0(w):
+        a,f=sets[w]
+        return go(rcopy(a,f.at[s],c0s.at[w],c0r.at[w],mate))
+    def piece(w,dz,quarter,cols=None):
+        a,f=sets[w]; Q=a.shape[0]//4
+        sp=((z+4-dz)%4)*2+c
+        rows=pl.ds(pl.multiple_of(quarter*Q,8),Q)
+        return f.at[sp,rows] if cols is None else f.at[sp,rows,cols]
+    def fwd(w,dz,kind,quarter,dev,cols=None):
+        ref=piece(w,dz,quarter,cols)
+        return go(rcopy(ref,ref,ss.at[w,kind,dz-1],rs.at[w,kind,dz-1],dev))
+    zc={};xc={};yc={};rc={}
+    def stage_z(w):
+        for dz in (1,2,3):
+            zc[w][dz-1].wait_recv()
+            xc[w,dz]=fwd(w,dz,1,r,xm)
+            yc[w,dz]=fwd(w,dz,2,r,ym)
+            fwd(w,dz,3,r,mate)
+    def stage_xy(w):
+        for dz in (1,2,3):
+            xc[w,dz].wait_recv()
+            rc[w,dz,0]=fwd(w,dz,6,p["rx"],ym,pl.ds(H,H))
+            fwd(w,dz,4,p["rx"],mate)
+            yc[w,dz].wait_recv()
+            rc[w,dz,1]=fwd(w,dz,7,p["ry"],xm,pl.ds(0,H))
+            fwd(w,dz,5,p["ry"],mate)
+    def stage_r(w):
+        for dz in (1,2,3):
+            rc[w,dz,0].wait_recv()
+            rc[w,dz,1].wait_recv()
+            fwd(w,dz,8,p["rd"],mate)
+    N=len(sets)
+    zc[0]=zsend(0); cores=[core0(0)]
+    for w in range(N):
+        stage_z(w)
+        if w+1<N:
+            zc[w+1]=zsend(w+1); cores.append(core0(w+1))
+        if w>0: stage_r(w-1)
+        if w==0:
+            for cp in vcs: cp.wait_recv()
+            vp[...]=v_ref[...]+vz[0]+vz[1]+vz[2]
+            vc=go(rcopy(vp,vm,vs.at[3],vr.at[3],mate))
+        stage_xy(w)
+    stage_r(N-1)
+    vc.wait_recv()
+    vf[...]=vp[...]+vm[...]
+    for w in range(N):
+        cores[w].wait_recv()
+        for dz in (1,2,3):
+            for kind,quarter in ((3,r),(4,p["rx"]),(5,p["ry"]),(8,p["rd"])):
+                ref=piece(w,dz,quarter)
+                rcopy(ref,ref,ss.at[w,kind,dz-1],rs.at[w,kind,dz-1],mate).wait_recv()
+    for cp in done: cp.wait_send()
+    for cp in locs: cp.wait()
+
+def gather_all(q,o,u,d,v):
+    S=8
+    any_=pl.BlockSpec(memory_space=pl.ANY); vm_=pl.BlockSpec(memory_space=pltpu.VMEM)
+    full=lambda a: jax.ShapeDtypeStruct((S,)+a.shape,a.dtype)
+    dma=pltpu.SemaphoreType.DMA
+    outs=pl.pallas_call(gather_kernel,in_specs=[any_]*4+[vm_],out_specs=[any_]*4+[vm_],
+      out_shape=[full(q),full(o),full(u),full(d),jax.ShapeDtypeStruct(v.shape,F32)],
+      scratch_shapes=[pltpu.VMEM((3,)+v.shape,F32),pltpu.VMEM(v.shape,F32),pltpu.VMEM(v.shape,F32),
+        dma((4,)),dma((4,)),dma((4,)),dma((4,9,3)),dma((4,9,3)),dma((4,)),dma((4,))],
+      compiler_params=pltpu.CompilerParams(collective_id=1,has_side_effects=True),name="gather_all")(q,o,u,d,v)
+    return [a.reshape(-1,a.shape[-1]) for a in outs[:4]]+[outs[4]]
+
+def reduce_kernel(nset,*refs):
+    g=refs[:nset]; v_ref=refs[nset]
+    outs=refs[nset+1:2*nset+1]; vo=refs[2*nset+1]
+    sc=list(refs[2*nset+2:])
+    take=lambda n: [sc.pop(0) for _ in range(n)]
+    acc=take(nset); cb=take(nset); a1=take(nset); b1=take(nset); a2=take(nset); b2=take(nset); zb=take(nset); fin=take(nset)
+    vb,lsem,ss,rs,vs,vr,osem=take(7)
+    p=place()
+    greet(p)
+    r,s,c,z,x,y=p["r"],p["s"],p["c"],p["z"],p["x"],p["y"]
+    mate=(r,p["mate"]); xm=(p["rx"],s); ym=(p["ry"],s)
+    zdev=[(r,zpeer(p,dz)*2+c) for dz in (1,2,3)]
+    H=acc[0].shape[-1]//2
+    lo=pl.ds(0,H); hi=pl.ds(H,H)
+    done=[]
+    def go(cp):
+        cp.start(); done.append(cp); return cp
+    cp_={}
+    loc={}
+    def C(k):
+        cp_[k,0]=go(rcopy(g[k].at[:,1-c],cb[k],ss.at[k,0],rs.at[k,0],mate))
+        loc[k]=pltpu.make_async_copy(g[k].at[:,c],acc[k],lsem.at[k]); loc[k].start()
+    def X(k):
+        loc[k].wait()
+        cp_[k,0].wait_recv()
+        def add(i,t):
+            acc[k][i]=acc[k][i]+cb[k][i]
+            return t
+        lax.fori_loop(0,4,add,0)
+        for yy in range(2):
+            cp_[k,1+yy]=go(rcopy(acc[k].at[:,yy*2+1-x,:,lo],a1[k].at[:,yy],ss.at[k,1+yy],rs.at[k,1+yy],xm))
+        cp_[k,3]=go(rcopy(acc[k].at[:,pl.ds((1-y)*2,2),:,hi],b1[k],ss.at[k,3],rs.at[k,3],ym))
+    def Y(k):
+        cp_[k,1].wait_recv(); cp_[k,2].wait_recv(); cp_[k,3].wait_recv()
+        def add(i,t):
+            for yy in range(2):
+                acc[k][i,yy*2+x,:,lo]=acc[k][i,yy*2+x,:,lo]+a1[k][i,yy]
+            for xx in range(2):
+                acc[k][i,y*2+xx,:,hi]=acc[k][i,y*2+xx,:,hi]+b1[k][i,xx]
+            return t
+        lax.fori_loop(0,4,add,0)
+        cp_[k,4]=go(rcopy(acc[k].at[:,(1-y)*2+x,:,lo],a2[k],ss.at[k,4],rs.at[k,4],ym))
+        cp_[k,5]=go(rcopy(acc[k].at[:,y*2+1-x,:,hi],b2[k],ss.at[k,5],rs.at[k,5],xm))
+    def Z(k):
+        cp_[k,4].wait_recv(); cp_[k,5].wait_recv()
+        def add(i,t):
+            acc[k][i,r,:,lo]=acc[k][i,r,:,lo]+a2[k][i]
+            acc[k][i,r,:,hi]=acc[k][i,r,:,hi]+b2[k][i]
+            return t
+        lax.fori_loop(0,4,add,0)
+        for dz in (1,2,3):
+            cp_[k,5+dz]=go(rcopy(acc[k].at[zpeer(p,dz),r],zb[k].at[dz-1],ss.at[k,5+dz],rs.at[k,5+dz],zdev[dz-1]))
+    def Fn(k):
+        for dz in (1,2,3): cp_[k,5+dz].wait_recv()
+        t=acc[k][z,r].astype(F32)
+        for dz in range(3): t=t+zb[k][dz].astype(F32)
+        fin[k][r]=t.astype(BF)
+        cp_[k,9]=go(rcopy(fin[k].at[r],fin[k].at[r],ss.at[k,9],rs.at[k,9],xm))
+        cp_[k,10]=go(rcopy(fin[k].at[r],fin[k].at[r],ss.at[k,10],rs.at[k,10],ym))
+    def G(k):
+        cp_[k,9].wait_recv()
+        cp_[k,11]=go(rcopy(fin[k].at[p["rx"],:,hi],fin[k].at[p["rx"],:,hi],ss.at[k,11],rs.at[k,11],ym))
+        cp_[k,10].wait_recv()
+        cp_[k,12]=go(rcopy(fin[k].at[p["ry"],:,lo],fin[k].at[p["ry"],:,lo],ss.at[k,12],rs.at[k,12],xm))
+    def Hh(k):
+        cp_[k,11].wait_recv(); cp_[k,12].wait_recv()
+        loc["o",k]=pltpu.make_async_copy(fin[k],outs[k],osem.at[k]); loc["o",k].start()
+    zz=(z//2)*2
+    vdev=[mate,xm,ym,(r,(zz+1-z%2)*2+c),(r,((z+2)%4)*2+c)]
+    def V(n):
+        if n>0:
+            cp_["v",n-1].wait_recv()
+        if n==0: vb[0]=v_ref[...]
+        else: vb[2*n]=vb[2*n-2]+vb[2*n-1]
+        if n<5:
+            cp_["v",n]=go(rcopy(vb.at[2*n],vb.at[2*n+1],vs.at[n],vr.at[n],vdev[n]))
+        else:
+            vo[...]=vb[10]
+    stages=[C,X,Y,Z,Fn,G,Hh]
+    for t in range(nset+6):
+        if t==0: C(0)
+        if t<6: V(t)
+        if t+1<nset: C(t+1)
+        for si in range(1,7):
+            k=t-si+1
+            if 0<=k<nset: stages[si](k)
+    for cp in done: cp.wait_send()
+    for k in range(nset): loc["o",k].wait()
+
+def reduce_all(gs,v):
+    n=len(gs)
+    any_=pl.BlockSpec(memory_space=pl.ANY); vm_=pl.BlockSpec(memory_space=pltpu.VMEM)
+    dma=pltpu.SemaphoreType.DMA
+    D=gs[0].shape[1]
+    Qs=[a.shape[0]//32 for a in gs]
+    g5=[a.reshape(4,2,4,q,D) for a,q in zip(gs,Qs)]
+    H=D//2
+    V=pltpu.VMEM
+    scr=[V((4,4,q,D),BF) for q in Qs]+[V((4,4,q,D),BF) for q in Qs]+[V((4,2,q,H),BF) for q in Qs]*1+[V((4,2,q,H),BF) for q in Qs]
+    scr+=[V((4,q,H),BF) for q in Qs]+[V((4,q,H),BF) for q in Qs]+[V((3,q,D),BF) for q in Qs]+[V((4,q,D),BF) for q in Qs]
+    scr+=[V((11,)+v.shape,F32),dma((n,)),dma((n,13)),dma((n,13)),dma((5,)),dma((5,)),dma((n,))]
+    outs=pl.pallas_call(functools.partial(reduce_kernel,n),in_specs=[any_]*n+[vm_],out_specs=[any_]*n+[vm_],
+      out_shape=[jax.ShapeDtypeStruct((4,q,D),BF) for q in Qs]+[jax.ShapeDtypeStruct(v.shape,F32)],
+      scratch_shapes=scr,compiler_params=pltpu.CompilerParams(collective_id=2,has_side_effects=True,vmem_limit_bytes=56<<20),name="reduce_all")(*g5,v)
+    return [a.reshape(-1,D) for a in outs[:n]],outs[n]
+
 
 def gather(x):
     return lax.all_gather(x, "shard", axis=0, tiled=True)
 
 
-def reduce_shard(g):
-    part = lax.psum_scatter(g, "shard", scatter_dimension=0, tiled=True)
-    return lax.psum(part, "rep").astype(F32)
+def gather_plain(q, o, u, d, v):
+    return [gather(q), gather(o), gather(u), gather(d), lax.psum(v, "shard")]
+
+
+def reduce_plain(gs, v):
+    def one(g):
+        part = lax.psum_scatter(g, "shard", scatter_dimension=0, tiled=True)
+        return lax.psum(part, "rep")
+
+    return [one(g) for g in gs], lax.psum(v, ("rep", "shard"))
 
 
 def local(tokens, segment_ids, qkv_weight, out_weight, up_weight, down_weight,
@@ -314,16 +529,13 @@
     cot = cotangent[0]
     seg = segment_ids[0]
     model = tok.shape[1]
-    shards = lax.axis_size("shard")
-    width = qkv_weight.shape[1]
-    vec_part = jnp.stack([norm1_gain, norm1_shift, norm2_gain, norm2_shift])
-    vec_rows = jnp.zeros((8, model), BF).at[:4, : vec_part.shape[1]].set(vec_part)
-    first = gather(jnp.concatenate([qkv_weight.T, vec_rows], axis=0)).reshape(shards, width + 8, model)
-    qkv_t = first[:, :width].reshape(shards * width, model)
-    vec = first[:, width:, : vec_part.shape[1]].transpose(1, 0, 2).reshape(8, model).astype(F32)
-    out_full = gather(out_weight)
-    up_t = gather(up_weight.T)
-    down_full = gather(down_weight)
+    known = lax.axis_size("rep") == 4 and lax.axis_size("shard") == 8
+    piece = norm1_gain.shape[0]
+    at = lax.axis_index("shard") * piece
+    vec_part = jnp.stack([norm1_gain, norm1_shift, norm2_gain, norm2_shift]).astype(F32)
+    vec_mine = lax.dynamic_update_slice(jnp.zeros((8, model), F32), vec_part, (0, at))
+    collect = gather_all if known else gather_plain
+    qkv_t, out_full, up_t, down_full, vec = collect(qkv_weight.T, out_weight, up_weight.T, down_weight, vec_mine)
     segc, segr, nst, nblk = prep(seg)
     normed, projected = qkv_proj(tok, qkv_t, vec)
     attended, lse, bias, sig = attn_fwd(projected, segc, segr, nst, nblk, unroll=6)
@@ -331,14 +543,12 @@
     gproj = attn_bwd(projected, gatt, attended, lse, bias, sig, nblk, unroll=5)
     gqkv = qkv_wgrad(gproj, normed)
     tgrad, vec1 = qkv_dgrad(gproj, qkv_t, tok, gres, vec)
-    down_grad = reduce_shard(gdn)
-    up_grad = reduce_shard(gup).T
-    out_grad = reduce_shard(gow)
-    qkv_grad = reduce_shard(gqkv).T
-    vec_all = lax.psum(jnp.concatenate([vec1[:2], vec2[:2]], axis=0), ("rep", "shard"))
-    piece = norm1_gain.shape[0]
-    mine = lax.dynamic_slice_in_dim(vec_all, lax.axis_index("shard") * piece, piece, 1)
-    return (output[None], tgrad[None], qkv_grad, out_grad, up_grad, down_grad,
+    vec_all = jnp.concatenate([vec1[:2], vec2[:2], jnp.zeros((4, model), F32)], axis=0)
+    spread = reduce_all if known else reduce_plain
+    grads, vec_sum = spread([gdn, gup, gow, gqkv], vec_all)
+    down_grad, up_grad, out_grad, qkv_grad = [g.astype(F32) for g in grads]
+    mine = lax.dynamic_slice_in_dim(vec_sum, at, piece, 1)
+    return (output[None], tgrad[None], qkv_grad.T, out_grad, up_grad.T, down_grad,
             mine[0], mine[1], mine[2], mine[3])
 
 

time: 520 us -> 318 us (0.61); the launches traced: 510 us -> 314 us
  waiting for transfers between devices: 300 us -> 0 us
  Pallas kernels: 117 us -> 279 us
  blocking collectives: 38.2 us -> 0 us
  between operations: 14.5 us -> 1.13 us
  local copies, waits for them, and re-layouts: 33.3 us -> 27.9 us
    pallas_call x0 -> x2, Pallas kernels: none -> 164 us  [the longest x1 98.4 us: reduce_all(): pl.pallas_call(functools.partial(reduce_kernel, n), in_specs=[any_] * n +...]
    reduce_scatter x4 -> x0, waiting for transfers between devices: 153 us -> none  [reduce_shard(): part = lax.psum_scatter(g, 'shard', scatter_dimension=0, tiled=True)]
    all_gather x4 -> x0, waiting for transfers between devices: 129 us -> none  [gather(): return lax.all_gather(x, 'shard', axis=0, tiled=True)]
    psum x1 -> x0, blocking collectives: 38.2 us -> none  [local(): lax.psum(jnp.concatenate([vec1[:2], vec2[:2]], axis=0), ('rep', 'shard'))]
    psum x1 -> x0, waiting for transfers between devices: 14.7 us -> none  [reduce_shard(): return lax.psum(part, 'rep').astype(F32)]
    unnamed x50 -> x47, local copies, waits for them, and re-layouts: 26.5 us -> 23.7 us
  transfers between devices with their start and end apart: 9 -> 0, of which waited for: 7 -> 0; matrix products, arithmetic and copies ran while one was open for 2% -> 0% of each run, Pallas kernels for 13% -> 0%
where the time goes in v2:
time: 318 us; the launch traced here: 314 us
  Pallas kernels  279 us (88%)
  local copies, waits for them, and re-layouts  27.9 us (9%)
  other arithmetic  6.05 us (2%)
    pallas_call x1, Pallas kernels, reduce_all(): pl.pallas_call(functools.partial(reduce_kernel, n), in_specs=[any_] * n +...  98.4 us
    pallas_call x1, Pallas kernels, gather_all(): pl.pallas_call(gather_kernel, in_specs=[any_] * 4 + [vm_], out_specs=[any...  65.4 us
    pallas_call x1, Pallas kernels, mlp(): pl.pallas_call(functools.partial(mlp_kernel, NR, F // C, C, R), grid=(NR...  49.9 us
    pallas_call x1, Pallas kernels, attn_bwd(): pl.pallas_call(functools.partial(attn_bwd_kernel, BQ, G, NW, HP, unroll,...  27 us
    unnamed x47, local copies, waits for them, and re-layouts  23.7 us
    pallas_call x1, Pallas kernels, attn_fwd(): pl.pallas_call(functools.partial(attn_fwd_kernel, BQ, G, NW, HP, unroll),...  20.3 us
    pallas_call x1, Pallas kernels, qkv_dgrad(): pl.pallas_call(dg_kernel, grid=(T // R,), in_specs=[rb(E), c((E, D)), rb(...  6.93 us

profile of v2, /device:TPU:0, one launch (start us, length us, event | category | flops | bytes accessed | tf_op | source)
XLA Modules:
  0.0 313.8 jit_solution(17388090163686513185)
XLA Ops:
  0.7 0.8 maximum_convert_fusion
  1.9 2.1 copy.26
  4.0 65.4 %gather_all.1 = (bf16[8,288,768]{2,1,0:T(8,128)(2,1)}, bf16[8,96,768]{2,1,0:T(8,128)(2,1)}, bf16[8,384,768]{2,1,0:T(8,128)(2,1)}, bf16[8,384,768]{2,1,0:T(8,128)(2,1)}, f32[8,768]{1,0:T(8,128)}) custom-call(bf16[288,768]{1,0:T(8,128)(2,1)} %bitcast.61, bf16[96,768]{1,0:T(8,128)(2,1)} %o_ref.1, bf16[384,768]{1,0:T(8,128)(2,1)} %bitcast.56, ...), custom_call_target="tpu_custom_call" | custom-call | tf_op jit(solution)/shard_map/gather_all/pallas_call | solution.py:396
  69.5 2.0 copy-done.4
  71.5 0.7 copy-done.17
  72.2 5.3 %qkv_proj.1 = (bf16[1024,768]{1,0:T(8,128)(2,1)S(1)}, bf16[1024,2304]{1,0:T(8,128)(2,1)S(1)}) custom-call(bf16[1024,768]{1,0:T(8,128)(2,1)S(1)} %bitcast.47, bf16[2304,768]{1,0:T(8,128)(2,1)S(1)} %bitcast.43, f32[8,768]{1,0:T(8,128)S(1)} %copy-done.17), custom_call_target="tpu_custom_call" | custom-call | tf_op jit(solution)/shard_map/qkv_proj/pallas_call | solution.py:207
  77.5 2.2 copy-done.2
  80.4 2.3 copy-done.3
  82.8 20.3 %attn_fwd.1 = (bf16[1024,768]{1,0:T(8,128)(2,1)S(1)}, f32[1024,128]{1,0:T(8,128)S(1)}, f32[8,128,640]{2,1,0:T(8,128)S(1)}, bf16[8,128,640]{2,1,0:T(8,128)(2,1)S(1)}) custom-call(s32[8]{0:T(128)S(1)} %and_select_fusion.nblk_ref, bf16[1024,2304]{1,0:T(8,128)(2,1)S(1)} %copy-done.3, s32[1024,1]{1,0:T(8,128)S(1)} %copy.27.segc_ref, s32[1,1024]{1,0:T(1,128)S(1)} %copy-done.19, ...), custom_call_target="tpu_custom_call" | custom-call | tf_op jit(solution)/shard_map/attn_fwd/pallas_call | solution.py:94
  103.1 1.1 copy-done.9
  104.2 1.5 copy-done.11
  105.7 1.0 copy-done.13
  106.7 0.8 copy-done.15
  107.5 49.9 %mlp.1 = (bf16[1024,768]{1,0:T(8,128)(2,1)}, f32[1024,768]{1,0:T(8,128)}, bf16[1024,768]{1,0:T(8,128)(2,1)}, bf16[3072,768]{1,0:T(8,128)(2,1)}, bf16[3072,768]{1...) custom-call(bf16[1024,768]{1,0:T(8,128)(2,1)} %bitcast.46, bf16[1024,768]{1,0:T(8,128)(2,1)} %copy-done.9, ...), custom_call_target="tpu_custom_call" | custom-call | tf_op jit(solution)/shard_map/mlp/pallas_call | solution.py:268
  157.4 1.4 copy-done.12
  158.8 1.3 copy-done.14
  160.1 1.0 copy-done.16
  161.2 27.0 %attn_bwd.1.gp_ref = bf16[1024,2304]{1,0:T(8,128)(2,1)} custom-call(s32[8]{0:T(128)S(1)} %and_select_fusion.nblk_ref, bf16[1024,2304]{1,0:T(8,128)(2,1)} %copy-done.2, bf16[1024,768]{1,0:T(8,128)(2,1)S(1)} %copy-done.12, bf16[1024,768]{1,0:T(8,128)(2,1)} %copy-done.9, f32[1024,128]{1,0:T(8,128)S(1)} %copy-done.16, f32[8,128,640]{2,1,0:T(8,128)} %copy-done.11, ...), custom_call_target="tpu_custom_call" | custom-call | tf_op jit(solution)/shard_map/attn_bwd/pallas_call | solution.py:177
  188.2 2.3 copy-done
  190.5 1.9 copy-done.10
  192.4 6.9 %qkv_dgrad.1 = (bf16[1024,768]{1,0:T(8,128)(2,1)}, f32[8,768]{1,0:T(8,128)S(1)}) custom-call(bf16[1024,2304]{1,0:T(8,128)(2,1)S(1)} %copy-done, bf16[2304,768]{1,0:T(8,128)(2,1)S(1)} %bitcast.44, bf16[1024,768]{1,0:T(8,128)(2,1)S(1)} %bitcast.48, f32[1024,768]{1,0:T(8,128)S(1)} %copy-done.10, f32[8,768]{1,0:T(8,128)S(1)} %copy-done.18), custom_call_target="tpu_custom_call" | custom-call | tf_op jit(solution)/shard_map/qkv_dgrad/pallas_call | solution.py:298
  199.4 0.7 slice.33
  200.2 0.7 maximum_maximum_fusion.refs_4_
  200.9 5.5 %qkv_wgrad.1 = bf16[2304,768]{1,0:T(8,128)(2,1)S(1)} custom-call(bf16[1024,2304]{1,0:T(8,128)(2,1)S(1)} %copy-done.1, bf16[1024,768]{1,0:T(8,128)(2,1)S(1)} %get-tuple-element.52.n_ref), custom_call_target="tpu_custom_call" | custom-call | tf_op jit(solution)/shard_map/qkv_wgrad/pallas_call | solution.py:280
  206.4 1.8 copy-done.6
  208.2 98.4 %reduce_all.1 = (bf16[4,96,768]{2,1,0:T(8,128)(2,1)}, bf16[4,96,768]{2,1,0:T(8,128)(2,1)}, bf16[4,24,768]{2,1,0:T(8,128)(2,1)}, bf16[4,72,768]{2,1,0:T(8,128)(2,1)}, f32[8,768]{1,0:T(8,128)}) custom-call(bf16[4,2,4,96,768]{4,3,2,1,0:T(8,128)(2,1)} %bitcast.52, bf16[4,2,4,96,768]{4,3,2,1,0:T(8,128)(2,1)} %bitcast.53, bf16[4,2,4,24,768]{4,3,2,1,0:T(8,128)(2,1)} %bitcast.60, ...), custom_call_target="tpu_custom_call" | custom-call | tf_op jit(solution)/shard_map/reduce_all/pallas_call | solution.py:504
  306.6 2.4 bitcast_convert_fusion
  309.1 1.4 copy.28
  310.5 1.0 convert_bitcast_fusion
  311.5 0.7 bitcast_convert_fusion.2
  312.2 0.8 constant_dynamic-slice_fusion
  313.0 0.5 slice_bitcast_fusion
  (43 shorter events, 1.2 us)
Async XLA Ops:
  0.6 68.8 %copy-start.7 = (bf16[1,1024,768]{2,1,0:T(8,128)(2,1)S(1)}, bf16[1,1024,768]{2,1,0:T(8,128)(2,1)}, u32[]{:S(2)}) copy-start(bf16[1,1024,768]{2,1,0:T(8,128)(2,1)} %param.11) | copy-start | bytes 4718596
  1.9 2.1 copy-start.22
  69.5 2.0 copy-start.4
  71.5 0.7 copy-start.17
  72.2 7.5 %copy-start.19 = (s32[1,1024]{1,0:T(1,128)S(1)}, s32[1,1024]{1,0:T(1,128)}, u32[]{:S(2)}) copy-start(s32[1,1024]{1,0:T(1,128)} %segr_ref.1) | copy-start | bytes 12292
  77.5 2.2 copy-start.2
  80.4 2.3 copy-start.3
  103.0 1.1 copy-start.9
  104.2 1.5 copy-start.11
  105.7 1.1 copy-start.13
  106.7 0.8 copy-start.15
  157.4 1.4 copy-start.12
  158.8 1.3 copy-start.14
  160.1 1.0 copy-start.16
  161.2 27.0 %copy-start.5 = (bf16[8,288,768]{2,1,0:T(8,128)(2,1)S(1)}, bf16[8,288,768]{2,1,0:T(8,128)(2,1)}, u32[]{:S(2)}) copy-start(bf16[8,288,768]{2,1,0:T(8,128)(2,1)} %get-tuple-element.35) | copy-start | bytes 10616836
  161.2 27.0 %copy-start.8 = (bf16[1,1024,768]{2,1,0:T(8,128)(2,1)S(1)}, bf16[1,1024,768]{2,1,0:T(8,128)(2,1)}, u32[]{:S(2)}) copy-start(bf16[1,1024,768]{2,1,0:T(8,128)(2,1)} %param.11) | copy-start | bytes 4718596
  161.2 27.0 %copy-start.18 = (f32[8,768]{1,0:T(8,128)S(1)}, f32[8,768]{1,0:T(8,128)}, u32[]{:S(2)}) copy-start(f32[8,768]{1,0:T(8,128)} %get-tuple-element.36.vec_ref) | copy-start | bytes 73732
  188.2 2.3 copy-start
  190.5 1.9 copy-start.10
  192.4 8.4 %copy-start.1 = (bf16[1024,2304]{1,0:T(8,128)(2,1)S(1)}, bf16[1024,2304]{1,0:T(8,128)(2,1)}, u32[]{:S(2)}) copy-start(bf16[1024,2304]{1,0:T(8,128)(2,1)} %attn_bwd.1.gp_ref) | copy-start | bytes 14155780
  206.4 1.9 copy-start.6
  309.1 1.4 copy-start.20
  309.1 2.4 copy-start.21
